TPU v7x, 256 devices: a whole 4x4x8 slice. The times are simulated.
256 devices in a mesh: plane: 4 (over z_hi), mode: 64 (over x, y, z_lo, core).
Axes of the slice: x: 4, y: 4, z: 8 (z_hi: 4, z_lo: 2; z = z_hi * 2 + z_lo), core: 2. Of those that a mesh axis runs over, the one named last changes fastest.
Arguments:
- phase_masks: float32 [4, 512, 512], P('plane'), may hold values from -3.140625 to 3.140625
- hg_orders: int32 [256, 2], P('mode'), may hold values from 0 to 44
- spot_index: int32 [256], P('mode'), may hold values from 0 to 1023
Outputs:
- phase_next: float32 [4, 512, 512], P('plane')
Inputs may be any that keep to these rules, and one draw needn't show every extreme that they name: `spot_index`: the output spot of each mode; several modes may share a spot.
All inputs are finite; a program needn't handle non-finite values.
Results may differ from a plain program's by a relative error of at most 0.018.
Values may be sent and summed in bfloat16 or wider, within the bound.
No kernel may reach another device: no remote copies, remote signals or barrier semaphores. Data moves between devices by JAX's collectives and lax.ppermute only.
A program may use at most 64 MiB of HBM per device.

v0:
```python
import math

import jax
import jax.numpy as jnp
from jax import lax
from jax.sharding import Mesh
from jax.sharding import PartitionSpec as P

ORDERS = 45
SPOT_SIDE = 32
MODE = ("mode_0", "mode_1", "mode_2", "mode_3")


CHIRP_RATE = math.pi / 48.0 * (math.pi / 48.0)
AMPLITUDE = 12.0
EPSILON = 1e-06


def cut_along(x, dim, count):
    shape = x.shape
    pieces = x.reshape(*shape[:dim], count, shape[dim] // count, *shape[dim + 1 :])
    return jnp.moveaxis(pieces, dim, 0)


def summed_on_arrival(x, axis, dim):
    pieces = cut_along(x, dim, lax.axis_size(axis))
    arrived = lax.all_to_all(pieces, axis, split_axis=0, concat_axis=0, tiled=True)
    return arrived.astype(jnp.float32).sum(axis=0)


def rows_for(lines, count):
    spare = -len(lines) % count
    return jnp.pad(lines, [(0, spare)] + [(0, 0)] * (lines.ndim - 1))


def from_everyone(x, axis):
    count = lax.axis_size(axis)
    return lax.all_to_all(jnp.broadcast_to(x[None], (count, *x.shape)), axis, 0, 0, tiled=True)


def laid_out(pieces, dim):
    pieces = jnp.moveaxis(pieces, 0, dim)
    shape = pieces.shape
    return pieces.reshape(*shape[:dim], shape[dim] * shape[dim + 1], *shape[dim + 2 :])


def gathered_by_axis(x, axes, dim):
    far, near = axes
    initial = from_everyone(x, far)
    pieces = jnp.swapaxes(from_everyone(initial, near), 0, 1)
    return laid_out(pieces.reshape(-1, *x.shape), dim)


def sent_and_summed(x, axis, dim):
    pieces = cut_along(x, dim, lax.axis_size(axis))
    arrived = lax.all_to_all(pieces, axis, split_axis=0, concat_axis=0, tiled=True)
    return arrived.sum(axis=0)


def sum_in_two_steps(x, axes, dim):
    far, near = axes
    own = sent_and_summed(cut_along(x, dim, lax.axis_size(far)), near, dim + 1)
    return jnp.sum(lax.all_to_all(own, far, 0, 0, tiled=True), axis=0)


def total_of(x, axes):
    lines = x.reshape(-1, x.shape[-1])
    padded = rows_for(lines, lax.axis_size(axes[0]) * lax.axis_size(axes[1]))
    whole = gathered_by_axis(sum_in_two_steps(padded, axes, 0), axes, 0)
    return lax.slice_in_dim(whole, 0, len(lines)).reshape(x.shape)


def kernel_parts(extent):
    positions = jnp.arange(extent, dtype=jnp.int32)
    centred = (positions + extent // 2) % extent - extent // 2
    wrapped = positions[:, None] * positions[None, :] % extent
    chirp_phase = CHIRP_RATE * (centred * centred).astype(jnp.float32)
    angles = 2.0 * math.pi / extent * wrapped.astype(jnp.float32) - chirp_phase[None, :]
    kernel_re = jnp.sum(jnp.cos(angles), axis=1) / extent
    kernel_im = jnp.sum(jnp.sin(angles), axis=1) / extent
    return (kernel_re, kernel_im)


def circulant(values):
    extent = values.shape[0]
    repeated = jnp.tile(values, extent + 1)
    hankel = repeated.reshape(extent, extent + 1)[:, :extent]
    return jnp.roll(jnp.flip(hankel, 1), 1, 1)


def operators(extent):
    kernel_re, kernel_im = kernel_parts(extent)
    matrix_re = circulant(kernel_re)
    matrix_im = circulant(kernel_im)
    prop_re = matrix_re.astype(jnp.bfloat16)
    prop_im = matrix_im.astype(jnp.bfloat16)
    forward_mats = (prop_re, prop_im, (matrix_re + matrix_im).astype(jnp.bfloat16))
    backward_mats = (prop_re, -prop_im, (matrix_re - matrix_im).astype(jnp.bfloat16))
    return (forward_mats, backward_mats)


def left_product(left_re, left_im, left_sum, field_re, field_im):
    field_sum = (field_re.astype(jnp.float32) + field_im.astype(jnp.float32)).astype(jnp.bfloat16)
    first_term = jnp.dot(left_re, field_re, preferred_element_type=jnp.float32)
    second_term = jnp.dot(left_im, field_im, preferred_element_type=jnp.float32)
    third_term = jnp.dot(left_sum, field_sum, preferred_element_type=jnp.float32)
    return (first_term - second_term, third_term - first_term - second_term)


def right_product(field_re, field_im, right_re, right_im, right_sum):
    field_sum = (field_re.astype(jnp.float32) + field_im.astype(jnp.float32)).astype(jnp.bfloat16)
    first_term = jnp.dot(field_re, right_re, preferred_element_type=jnp.float32)
    second_term = jnp.dot(field_im, right_im, preferred_element_type=jnp.float32)
    third_term = jnp.dot(field_sum, right_sum, preferred_element_type=jnp.float32)
    return (first_term - second_term, third_term - first_term - second_term)


def propagate(field_re, field_im, matrices):
    matrix_re, matrix_im, matrix_sum = matrices
    middle_re, middle_im = left_product(matrix_re, matrix_im, matrix_sum, field_re, field_im)
    middle_re, middle_im = lax.optimization_barrier(
        (middle_re.astype(jnp.bfloat16), middle_im.astype(jnp.bfloat16))
    )
    return right_product(middle_re, middle_im, matrix_re, matrix_im, matrix_sum)


def hermite(orders, extent):
    scaled = (jnp.arange(extent, dtype=jnp.float32) - (extent - 1) / 2.0) / (extent / 48.0)
    lowest = math.pow(math.pi, -0.25) * jnp.exp(-0.5 * scaled * scaled)
    second = math.sqrt(2.0) * scaled * lowest
    chosen = jnp.where((orders == 0)[:, None], lowest[None, :], 0.0)
    chosen = jnp.where((orders == 1)[:, None], second[None, :], chosen)

    def advance(degree, carried):
        previous, current, picked = carried
        degree_f = degree.astype(jnp.float32)
        higher = (
            jnp.sqrt(2.0 / (degree_f + 1.0)) * scaled * current
            - jnp.sqrt(degree_f / (degree_f + 1.0)) * previous
        )
        picked = jnp.where((orders == degree + 1)[:, None], higher[None, :], picked)
        return (current, higher, picked)

    previous, current, chosen = lax.fori_loop(1, ORDERS - 1, advance, (lowest, second, chosen))
    return chosen


def spot_profile(spots, extent):
    coords = jnp.arange(extent, dtype=jnp.float32) - (extent - 1) / 2.0
    spacing = extent / 40.0
    spot_width = extent / 120.0
    centre = (SPOT_SIDE - 1) / 2.0
    spot_row = (spots // SPOT_SIDE).astype(jnp.float32) - centre
    spot_col = (spots % SPOT_SIDE).astype(jnp.float32) - centre
    offset_x = (coords[None, :] - spacing * spot_row[:, None]) / spot_width
    offset_y = (coords[None, :] - spacing * spot_col[:, None]) / spot_width
    return (jnp.exp(-offset_x * offset_x), jnp.exp(-offset_y * offset_y))


def mode_tables(orders, spots, extent):
    profile_x, profile_y = spot_profile(spots, extent)
    return (
        AMPLITUDE * hermite(orders[:, 0], extent),
        hermite(orders[:, 1], extent),
        profile_x,
        profile_y,
    )


def apply_mask(field_re, field_im, cos_mask, sin_mask):
    masked_re = (field_re * cos_mask - field_im * sin_mask).astype(jnp.bfloat16)
    masked_im = (field_re * sin_mask + field_im * cos_mask).astype(jnp.bfloat16)
    return lax.optimization_barrier((masked_re, masked_im))


def remove_mask(back_re, back_im, cos_mask, sin_mask):
    reply_re = (back_re * cos_mask + back_im * sin_mask).astype(jnp.bfloat16)
    reply_im = (back_im * cos_mask - back_re * sin_mask).astype(jnp.bfloat16)
    return lax.optimization_barrier((reply_re, reply_im))


def whole_mode(input_x, input_y, target, cos_masks, sin_masks, forward_mats, backward_mats):
    plane_count = cos_masks.shape[0]
    field_re = input_x[:, None] * input_y[None, :]
    field_im = jnp.zeros_like(field_re)
    masked_fields = []
    for plane_at in range(plane_count):
        masked_re, masked_im = apply_mask(
            field_re, field_im, cos_masks[plane_at], sin_masks[plane_at]
        )
        masked_fields.append((masked_re, masked_im))
        out_re, out_im = propagate(masked_re, masked_im, forward_mats)
        rounded = lax.optimization_barrier(
            (out_re.astype(jnp.bfloat16), out_im.astype(jnp.bfloat16))
        )
        field_re = rounded[0].astype(jnp.float32)
        field_im = rounded[1].astype(jnp.float32)
    coupling_re = jnp.sum(target * out_re)
    coupling_im = jnp.sum(target * out_im)
    source_re, source_im = lax.optimization_barrier(
        ((coupling_re * target).astype(jnp.bfloat16), (coupling_im * target).astype(jnp.bfloat16))
    )
    grad_terms = []
    for plane_at in reversed(range(plane_count)):
        back_re, back_im = propagate(source_re, source_im, backward_mats)
        masked_re, masked_im = masked_fields[plane_at]
        grad_terms.append(
            2.0
            * (back_im * masked_re.astype(jnp.float32) - back_re * masked_im.astype(jnp.float32))
        )
        source_re, source_im = remove_mask(
            back_re, back_im, cos_masks[plane_at], sin_masks[plane_at]
        )
    return jnp.stack(grad_terms[::-1])


def shards(phase_masks, hg_orders, spot_index):
    extent = phase_masks.shape[1]
    modes_here = hg_orders.shape[0]
    plane_count = lax.axis_size("plane")
    section_index = lax.axis_index("plane")
    forward_mats, backward_mats = operators(extent)
    all_masks = lax.all_gather(phase_masks, "plane", axis=0, tiled=True)
    cos_masks = jnp.cos(all_masks)
    sin_masks = jnp.sin(all_masks)
    per_section = modes_here // plane_count
    mode_start = section_index * per_section
    own_orders = lax.dynamic_slice_in_dim(hg_orders, mode_start, per_section, 0)
    own_spots = lax.dynamic_slice_in_dim(spot_index, mode_start, per_section, 0)
    own_tables = mode_tables(own_orders, own_spots, extent)

    def one_mode(mode_item, grad_total):
        picked_rows = [
            lax.dynamic_index_in_dim(entry_table, mode_item, 0, keepdims=False)
            for entry_table in own_tables
        ]
        target = picked_rows[2][:, None] * picked_rows[3][None, :]
        return grad_total + whole_mode(
            picked_rows[0],
            picked_rows[1],
            target,
            cos_masks,
            sin_masks,
            forward_mats,
            backward_mats,
        )

    grad_total = lax.fori_loop(
        0, per_section, one_mode, jnp.zeros((plane_count, extent, extent), jnp.float32)
    )
    local_sum = summed_on_arrival(grad_total.astype(jnp.bfloat16), "plane", 0)[0]
    summed = total_of(local_sum, (("mode_0", "mode_1", "mode_2"), "mode_3"))
    mean_square = jnp.mean(summed * summed)
    return (phase_masks[0] + summed / jnp.sqrt(mean_square + EPSILON))[None]


def solution(mesh):
    finer = Mesh(
        mesh.devices.reshape(mesh.shape["plane"], 4, 4, 2, 2),
        ("plane", "mode_0", "mode_1", "mode_2", "mode_3"),
    )
    placed = (P("plane", None, None), P(MODE, None), P(MODE))
    return jax.shard_map(
        shards, mesh=finer, in_specs=placed, out_specs=P("plane", None, None), check_vma=False
    )
```

profile of v0, /device:TPU:1, one launch (start us, length us, event | category | flops | bytes accessed | tf_op | source)
XLA Modules:
  0.0 260.7 jit_solution(12880406644514572669)
XLA Ops:
  6.5 0.7 all-gather.2.cloned.1.call-update
  7.3 0.6 fusion.111
  10.3 37.3 %while.45 = (s32[]{:T(128)}, f32[512]{0:T(512)S(1)}, f32[512]{0:T(512)S(1)}, f32[1,512]{1,0:T(1,128)S(1)}, s32[1]{0:T(128)}, /*index=5*/s32[]{:T(128)}, f32[]{:T(128)}, f32[]{:T(128)}, f32[]{:T(128)}, s32[]{:T(128)}) while((s32[]{:T(128)}, f32[512]{0:T(512)S(1)}, f32[512]{0:T(512)S(1)}, f32[1,512]{1,0:T(1,128)S(1)}, s32[1]{0:T(128)}, ...), condition=%wide.region_2.3_spmd.clone, body=%wide.region_1.2_spmd.clone.sunk | while | flops 3081 | bytes 20683 | solution.py:144
  47.7 33.8 %while.46 = (s32[]{:T(128)}, f32[512]{0:T(512)S(1)}, f32[512]{0:T(512)S(1)}, f32[1,512]{1,0:T(1,128)S(1)}, s32[1]{0:T(128)}, /*index=5*/s32[]{:T(128)}, f32[]{:T(128)}, f32[]{:T(128)}, f32[]{:T(128)}, s32[]{:T(128)}) while((s32[]{:T(128)}, f32[512]{0:T(512)S(1)}, f32[512]{0:T(512)S(1)}, f32[1,512]{1,0:T(1,128)S(1)}, s32[1]{0:T(128)}, ...), condition=%wide.region_4.5_spmd.clone, body=%wide.region_3.4_spmd.clone.sunk | while | flops 3081 | bytes 20683 | solution.py:144
  81.5 1.2 dynamic_slice.15
  85.3 5.0 %sine_reduce_fusion = (f32[512]{0:T(512)S(1)}, f32[512]{0:T(512)S(1)}) fusion(f32[512]{0:T(512)S(1)} %fusion.107), kind=kLoop, calls=%fused_computation.169 | loop fusion | flops 4455424 | bytes 6144 | tf_op jit(solution)/shard_map/reduce_sum | solution.py:80
  90.5 1.2 reshape_tile.7
  91.7 0.7 slice.92
  92.9 1.2 reshape_tile.6
  94.0 0.7 slice.88
  94.8 1.3 slice.89
  96.1 1.5 reverse.5
  97.9 1.5 reverse.4
  100.1 1.2 fusion.86
  101.3 0.6 subtract_convert_fusion.6
  102.0 16.0 %fusion.110 = (f32[4,512,512]{2,1,0:T(8,128)S(1)}, f32[4,512,512]{2,1,0:T(8,128)S(1)}) fusion(f32[4,512,512]{2,1,0:T(8,128)} %all-gather.2.cloned.1.call-done), kind=kLoop, calls=%fused_computation.222 | loop fusion | bytes 12582912 | tf_op jit(solution)/shard_map/sin | solution.py:225
  119.2 0.5 fusion.25
  120.6 0.4 fusion.26
  121.1 0.5 fusion.42
  122.4 0.5 fusion.27
  123.8 0.4 fusion.28
  124.2 0.5 fusion.50
  125.5 0.5 fusion.29
  126.9 0.4 fusion.30
  127.4 0.5 fusion.58
  128.7 0.5 fusion.31
  129.6 1.2 fusion.71
  130.8 1.2 fusion.77
  132.1 1.5 fusion.73
  134.4 0.5 fusion.32
  135.4 0.4 fusion.99
  135.8 0.9 subtract_convert_fusion.5
  137.6 0.5 fusion.33
  138.1 0.6 fusion.121
  139.2 0.9 subtract_convert_fusion.3
  140.9 0.5 fusion.34
  141.9 0.4 fusion.91
  142.3 0.9 subtract_convert_fusion.1
  144.1 0.5 fusion.35
  145.0 0.4 fusion.87
  145.5 0.7 fusion.37
  146.4 56.7 %all_to_all.25 = bf16[4,1,512,512]{3,2,1,0:T(8,128)(2,1)S(1)} all-to-all(bf16[4,1,512,512]{3,2,1,0:T(8,128)(2,1)S(1)} %pad_maximum_fusion), channel_id=1, replica_groups=mesh['plane'=4,'mode_0'=4,'mode_1'=4,'mode_2'=2,'mode_3'=2] {'plane'}, dimensions={0} | all-to-all | bytes 4194304 | tf_op jit(solution)/shard_map/all_to_all | solution.py:27
  203.5 8.1 %all_to_all.26 = f32[2,32,8,512]{3,2,1,0:T(8,128)S(1)} all-to-all(f32[2,32,8,512]{3,2,1,0:T(8,128)S(1)} %copy.6), channel_id=1, replica_groups=mesh['plane'=4,'mode_0'=4,'mode_1'=4,'mode_2'=2,'mode_3'=2] {'mode_3'}, dimensions={0} | all-to-all | bytes 2097152 | tf_op jit(solution)/shard_map/all_to_all | solution.py:56
  211.7 18.3 %all_to_all.27 = f32[32,8,512]{2,1,0:T(8,128)S(1)} all-to-all(f32[32,8,512]{2,1,0:T(8,128)S(1)} %reduce_sum.79), channel_id=1, replica_groups=mesh['plane'=4,'mode_0'=4,'mode_1'=4,'mode_2'=2,'mode_3'=2] {'mode_0','m..., dimensions={0} | all-to-all | bytes 1048576 | tf_op jit(solution)/shard_map/all_to_all | solution.py:63
  230.1 13.8 %all_to_all.28 = f32[32,8,512]{2,1,0:T(8,128)S(1)} all-to-all(f32[32,8,512]{2,1,0:T(8,128)S(1)} %broadcast_in_dim.155), channel_id=1, replica_groups=mesh['plane'=4,'mode_0'=4,'mode_1'=4,'mode_2'=2,'mode_3'=2] {'mode_0','m..., dimensions={0} | all-to-all | bytes 1048576 | tf_op jit(solution)/shard_map/all_to_all | solution.py:38
  244.0 7.0 %all_to_all.29 = f32[2,32,8,512]{3,2,1,0:T(8,128)S(1)} all-to-all(f32[2,32,8,512]{3,2,1,0:T(8,128)S(1)} %broadcast_in_dim.156), channel_id=1, replica_groups=mesh['plane'=4,'mode_0'=4,'mode_1'=4,'mode_2'=2,'mode_3'=2] {'mode_3'}, dimensions={0} | all-to-all | bytes 2097152 | tf_op jit(solution)/shard_map/all_to_all | solution.py:38
  251.0 0.9 multiply_reduce_fusion
  252.7 1.2 add.294
  (410 shorter events, 17.9 us)
Async XLA Ops:
  6.5 0.7 copy-start
  6.5 95.4 %all-gather.2.cloned.1.call-start = ((), (), s32[]{:S(2)}) async-start(), calls=%async_computation.5 | async-start | bytes 5242880 | tf_op jit(solution)/shard_map/all_gather | solution.py:223
  96.1 1.8 copy-start.3
  97.6 2.2 copy-start.4
  99.4 1.9 copy-start.5
  230.0 22.7 %copy-start.2 = (f32[1,512,512]{2,1,0:T(8,128)S(1)}, f32[1,512,512]{2,1,0:T(8,128)}, u32[]{:S(2)}) copy-start(f32[1,512,512]{2,1,0:T(8,128)} %param.7) | copy-start | bytes 3145732
  243.8 10.0 %copy-start.1 = (s32[4,2]{0,1:T(2,128)S(1)}, s32[4,2]{0,1:T(2,128)}, u32[]{:S(2)}) copy-start(s32[4,2]{0,1:T(2,128)} %param.8) | copy-start | bytes 100
Sparse Core Ops, SparseCore 0:
  9.1 75.9 all-gather.1
where the time goes:
time: 262 us; the launch traced here: 261 us
  blocking collectives  104 us (40%)
  loops' own time  68.2 us (26%)
  local copies, waits for them, and re-layouts  28 us (11%)
  matrix products  24.6 us (9%)
  between operations  19.6 us (7%)
  other arithmetic  15.8 us (6%)
    another operation x2, loops' own time, hermite(): lax.fori_loop(1, ORDERS - 1, advance, (lowest, second, chosen))  68.2 us
    all_to_all x1, blocking collectives, summed_on_arrival(): lax.all_to_all(pieces, axis, split_axis=0, concat_axis=0, tiled=True)  56.7 us
    all_to_all x2, blocking collectives, from_everyone(): lax.all_to_all(jnp.broadcast_to(x[None], (count, *x.shape)), axis, 0, 0,...  20.8 us
    all_to_all x1, blocking collectives, sum_in_two_steps(): return jnp.sum(lax.all_to_all(own, far, 0, 0, tiled=True), axis=0)  18.3 us
    sin x1, local copies, waits for them, and re-layouts, shards(): sin_masks = jnp.sin(all_masks)  16 us
    all_to_all x1, blocking collectives, sent_and_summed(): lax.all_to_all(pieces, axis, split_axis=0, concat_axis=0, tiled=True)  8.06 us
    dot_general x8, matrix products, right_product(): jnp.dot(field_sum, right_sum, preferred_element_type=jnp.float32)  5.82 us
  transfers between devices with their start and end apart: 1, of which 0 were waited for; matrix products, arithmetic and copies ran while one was open for 8% of the time, Pallas kernels for 0%

commit v1 on v0

v1 whole, which is shorter than its diff:
```python
import functools
import math

import jax
import jax.numpy as jnp
import numpy as np
from jax import lax
from jax.experimental import pallas as pl
from jax.experimental.pallas import tpu as pltpu
from jax.sharding import Mesh
from jax.sharding import PartitionSpec as P

ORDERS = 45
SPOT_SIDE = 32
MODE = ("mode_0", "mode_1", "mode_2", "mode_3")
XY = ("mode_0", "mode_1")
Z = ("plane", "mode_2")
CORE = "mode_3"
XY_DEVICES = 16
PLANES = 4
N = 512
B = 128
STRIP = 16
CHIRP_RATE = math.pi / 48.0 * (math.pi / 48.0)
AMPLITUDE = 12.0
EPSILON = 1e-06
F32 = jnp.float32
BF16 = jnp.bfloat16


def block_operators():
    f = np.arange(N)
    s = (f + N // 2) % N - N // 2
    chirp = np.exp(-1j * CHIRP_RATE * s.astype(np.float64) ** 2)
    phase = np.exp(2j * np.pi * ((f[:, None] * f[None, :]) % N) / N)
    kernel = (phase * chirp[None, :]).sum(axis=1) / N
    offset = np.arange(B)[:, None] - np.arange(B)[None, :]
    left, right = [], []
    for k in range(4):
        block = sum((-1j) ** (k * m) * kernel[(offset + B * m) % N] for m in range(4)) / 4.0
        real = np.block([[block.real, -block.imag], [block.imag, block.real]])
        left.append(real)
        right.append(real.T)
    to = lambda x: jnp.asarray(np.stack(x).astype(np.float32)).astype(BF16)
    return to(left), to(right)


def add(x, y):
    return (x[0] + y[0], x[1] + y[1])


def sub(x, y):
    return (x[0] - y[0], x[1] - y[1])


def turned(x, y):
    return (x[0] - y[1], x[1] + y[0])


def turned_back(x, y):
    return (x[0] + y[1], x[1] - y[0])


def dft4(x):
    a, b, c, d = add(x[0], x[2]), sub(x[0], x[2]), add(x[1], x[3]), sub(x[1], x[3])
    return [add(a, c), turned_back(b, d), sub(a, c), turned(b, d)]


def idft4(x):
    a, b, c, d = add(x[0], x[2]), sub(x[0], x[2]), add(x[1], x[3]), sub(x[1], x[3])
    return [add(a, c), turned(b, d), sub(a, c), turned_back(b, d)]


def both_ways(grid, transform):
    grid = [transform(row) for row in grid]
    cols = [transform([grid[k][l] for k in range(4)]) for l in range(4)]
    return [[cols[l][k] for l in range(4)] for k in range(4)]


def mul(x, y):
    return (x[0] * y[0] - x[1] * y[1], x[0] * y[1] + x[1] * y[0])


def dot(a, b):
    return jnp.dot(a, b, preferred_element_type=F32)


def lanes(l):
    return slice(l * B, (l + 1) * B)


def hermite_tables(psi):
    t = (lax.broadcasted_iota(jnp.int32, (8, N), 1).astype(F32) - (N - 1) / 2.0) / (N / 48.0)
    previous = math.pow(math.pi, -0.25) * jnp.exp(-0.5 * t * t)
    current = math.sqrt(2.0) * t * previous
    psi[0] = previous
    psi[1] = current
    for n in range(1, ORDERS - 1):
        higher = math.sqrt(2.0 / (n + 1.0)) * t * current - math.sqrt(n / (n + 1.0)) * previous
        psi[n + 1] = higher
        previous, current = current, higher


def spot_profile(index, shape, dim):
    coords = lax.broadcasted_iota(jnp.int32, shape, dim).astype(F32) - (N - 1) / 2.0
    centre = index.astype(F32) - (SPOT_SIDE - 1) / 2.0
    offset = (coords - (N / 40.0) * centre) / (N / 120.0)
    return jnp.exp(-offset * offset)


def split(x):
    high = x.astype(BF16)
    return high, (x - high.astype(F32)).astype(BF16)


def main_kernel(
    orders, spots, pick, half_own, half_other, left, right, keep, send,
    psi, source_x, far_x, x_ref, v_ref, y_ref, g_ref, mask_ref, tan_ref, grad, sems,
):
    mode, core = pick[0], pick[1]
    arrivals = [
        pltpu.make_async_copy(half_own, tan_ref.at[core], sems.at[0]),
        pltpu.make_async_copy(half_other, tan_ref.at[1 - core], sems.at[1]),
    ]
    for copy in arrivals:
        copy.start()
    hermite_tables(psi)
    source_y = psi[orders[mode, 1]]
    row = AMPLITUDE * psi[orders[mode, 0]][0:1]
    for k in range(4):
        source_x[k * B : (k + 1) * B, :] = jnp.broadcast_to(row[:, lanes(k)], (B, B)).T

    spot = spots[mode]
    down = spot_profile(spot // SPOT_SIDE, (N, B), 0)
    zero = jnp.zeros((B, B), F32)
    spread = dft4([(down[k * B : (k + 1) * B], zero) for k in range(4)])
    moved = []
    for k in range(4):
        high, low = split(jnp.concatenate(spread[k], axis=0))
        both = dot(left[k], jnp.concatenate([high, low], axis=1))
        total = both[:, :B] + both[:, B:]
        moved.append((total[:B], total[B:]))
    for k, part in enumerate(idft4(moved)):
        far_x[0, k * B : (k + 1) * B, :] = part[0]
        far_x[1, k * B : (k + 1) * B, :] = part[1]
    along = spot_profile(spot % SPOT_SIDE, (8, N), 1)
    zero = jnp.zeros((8, B), F32)
    spread = dft4([(along[:, lanes(l)], zero) for l in range(4)])
    moved = []
    for l in range(4):
        high, low = split(jnp.concatenate(spread[l], axis=1))
        both = dot(jnp.concatenate([high, low], axis=0), right[l])
        total = both[:8] + both[8:]
        moved.append((total[:, :B], total[:, B:]))
    far_y = idft4(moved)

    def rows_of(k, s):
        return pl.ds(k * B + s * STRIP, STRIP)

    def mask_at(plane, k, l, s):
        t = tan_ref[k // 2, (k % 2) * (B // STRIP) + s, plane, :, lanes(l)].astype(F32)
        twice = 2.0 / (1.0 + t * t)
        mask = (twice - 1.0, twice * t)
        if plane:
            mask_ref[plane - 1, 0, rows_of(k, s), lanes(l)] = mask[0]
            mask_ref[plane - 1, 1, rows_of(k, s), lanes(l)] = mask[1]
        return mask

    def kept_mask_at(plane, k, l, s):
        at = mask_ref.at[plane - 1]
        return (at[0, rows_of(k, s), lanes(l)], at[1, rows_of(k, s), lanes(l)])

    def spread_out(grid, s):
        grid = both_ways(grid, dft4)
        for k in range(4):
            for l in range(4):
                x_ref[k, pl.ds(s * STRIP, STRIP), lanes(l)] = grid[k][l][0].astype(BF16)
                x_ref[k, pl.ds(B + s * STRIP, STRIP), lanes(l)] = grid[k][l][1].astype(BF16)

    def gathered_up(s):
        grid = [
            [(y_ref[l, rows_of(k, s), 0:B], y_ref[l, rows_of(k, s), B : 2 * B]) for l in range(4)]
            for k in range(4)
        ]
        return both_ways(grid, idft4)

    def operate():
        for k in range(4):
            z = dot(left[k], x_ref[k]).astype(BF16)
            for l in range(4):
                v_ref[l, k * B : (k + 1) * B, 0:B] = z[:B, lanes(l)]
                v_ref[l, k * B : (k + 1) * B, B : 2 * B] = z[B:, lanes(l)]
        for l in range(4):
            y_ref[l] = dot(v_ref[l], right[l])

    def masked(plane, field, k, l, s):
        g = mul(field, mask_at(plane, k, l, s))
        g_ref[plane, 0, rows_of(k, s), lanes(l)] = g[0].astype(BF16)
        g_ref[plane, 1, rows_of(k, s), lanes(l)] = g[1].astype(BF16)
        return g

    def first_strip(s, carry):
        def at(k, l):
            field = source_x[rows_of(k, s), :] * source_y[0:1, lanes(l)]
            mask = mask_at(0, k, l, s)
            g = (field * mask[0], field * mask[1])
            g_ref[0, 0, rows_of(k, s), lanes(l)] = g[0].astype(BF16)
            g_ref[0, 1, rows_of(k, s), lanes(l)] = g[1].astype(BF16)
            return g

        spread_out([[at(k, l) for l in range(4)] for k in range(4)], s)
        return carry

    def forward_strip(plane, s, carry):
        field = gathered_up(s)
        spread_out([[masked(plane, field[k][l], k, l, s) for l in range(4)] for k in range(4)], s)
        return carry

    def last_strip(s, carry):
        field = gathered_up(s)
        carry = list(carry)
        for k in range(4):
            a = (far_x[0, rows_of(k, s), :], far_x[1, rows_of(k, s), :])
            for l in range(4):
                carry[l] = add(carry[l], mul(masked(PLANES - 1, field[k][l], k, l, s), a))
        return tuple(carry)

    def returned(plane, back, k, l, s):
        g = (
            g_ref[plane, 0, rows_of(k, s), lanes(l)].astype(F32),
            g_ref[plane, 1, rows_of(k, s), lanes(l)].astype(F32),
        )
        term = -2.0 * (back[0] * g[1] + back[1] * g[0])
        grad[k // 2, (k % 2) * (B // STRIP) + s, plane, :, lanes(l)] = term.astype(BF16)
        return mul(back, kept_mask_at(plane, k, l, s)) if plane else None

    strips = B // STRIP
    for copy in arrivals:
        copy.wait()
    lax.fori_loop(0, strips, first_strip, 0)
    for plane in range(1, PLANES - 1):
        operate()
        lax.fori_loop(0, strips, functools.partial(forward_strip, plane), 0)
    operate()
    nothing = jnp.zeros((STRIP, B), F32)
    sums = lax.fori_loop(0, strips, last_strip, tuple((nothing, nothing) for _ in range(4)))
    total = [mul((s[0][:8] + s[0][8:], s[1][:8] + s[1][8:]), y) for s, y in zip(sums, far_y)]
    coupling_re = jnp.sum(sum(t[0] for t in total))
    coupling_im = jnp.sum(sum(t[1] for t in total))
    back_y = [
        (coupling_re * y[0] + coupling_im * y[1], coupling_re * y[1] - coupling_im * y[0]) for y in far_y
    ]

    def turn_strip(s, carry):
        def at(k, l):
            a = (far_x[0, rows_of(k, s), :], far_x[1, rows_of(k, s), :])
            back = mul(a, (back_y[l][0][0:1], back_y[l][1][0:1]))
            return returned(PLANES - 1, back, k, l, s)

        spread_out([[at(k, l) for l in range(4)] for k in range(4)], s)
        return carry

    def backward_strip(plane, s, carry):
        back = gathered_up(s)
        reply = [[returned(plane, back[k][l], k, l, s) for l in range(4)] for k in range(4)]
        if plane:
            spread_out(reply, s)
        return carry

    lax.fori_loop(0, strips, turn_strip, 0)
    for plane in reversed(range(PLANES - 1)):
        operate()
        lax.fori_loop(0, strips, functools.partial(backward_strip, plane), 0)
    departures = [
        pltpu.make_async_copy(grad.at[core], keep, sems.at[0]),
        pltpu.make_async_copy(grad.at[1 - core], send, sems.at[1]),
    ]
    for copy in departures:
        copy.start()
    for copy in departures:
        copy.wait()


def main_call(orders, spots, pick, half_own, half_other, left, right):
    smem = pl.BlockSpec(memory_space=pltpu.SMEM)
    vmem = pl.BlockSpec(memory_space=pltpu.VMEM)
    hbm = pl.BlockSpec(memory_space=pl.ANY)
    half = (XY_DEVICES, PLANES, STRIP, N)
    return pl.pallas_call(
        main_kernel,
        name="modes",
        in_specs=[smem, smem, smem, hbm, hbm, vmem, vmem],
        out_specs=[hbm, hbm],
        out_shape=[jax.ShapeDtypeStruct(half, BF16)] * 2,
        scratch_shapes=[
            pltpu.VMEM((ORDERS, 8, N), F32),
            pltpu.VMEM((N, B), F32),
            pltpu.VMEM((2, N, B), F32),
            pltpu.VMEM((4, 2 * B, N), BF16),
            pltpu.VMEM((4, N, 2 * B), BF16),
            pltpu.VMEM((4, N, 2 * B), F32),
            pltpu.VMEM((PLANES, 2, N, N), BF16),
            pltpu.VMEM((PLANES - 1, 2, N, N), F32),
            pltpu.VMEM((2, *half), BF16),
            pltpu.VMEM((2, *half), BF16),
            pltpu.SemaphoreType.DMA((2,)),
        ],
    )(orders, spots, pick, half_own, half_other, left, right)


def tangent_kernel(where, phase, out):
    half_angle = 0.5 * phase[0]
    out[...] = (jnp.sin(half_angle) / jnp.cos(half_angle)).astype(BF16)


def tangent_call(where, phase_masks):
    return pl.pallas_call(
        tangent_kernel,
        name="tangent",
        grid_spec=pltpu.PrefetchScalarGridSpec(
            num_scalar_prefetch=1,
            grid=(1,),
            in_specs=[pl.BlockSpec((1, STRIP, N), lambda i, w: (0, w[0], 0))],
            out_specs=pl.BlockSpec((STRIP, N), lambda i, w: (0, 0)),
        ),
        out_shape=jax.ShapeDtypeStruct((STRIP, N), BF16),
    )(where, phase_masks)


def finish_kernel(pick, phase, own, other, out):
    squares = jnp.zeros((STRIP, N), F32)
    for g in range(XY_DEVICES):
        for part in (own, other):
            x = part[g].astype(F32)
            squares += x * x
    scale = lax.rsqrt(jnp.sum(squares, keepdims=True) / (N * N) + EPSILON)
    core = pick[1]
    for part, half in ((own, core), (other, 1 - core)):
        for g in range(XY_DEVICES):
            rows = pl.ds(half * (N // 2) + g * STRIP, STRIP)
            out[0, rows, :] = phase[0, rows, :] + part[g].astype(F32) * scale


def finish_call(pick, phase_masks, own, other):
    smem = pl.BlockSpec(memory_space=pltpu.SMEM)
    vmem = pl.BlockSpec(memory_space=pltpu.VMEM)
    return pl.pallas_call(
        finish_kernel,
        name="finish",
        in_specs=[smem, vmem, vmem, vmem],
        out_specs=vmem,
        out_shape=jax.ShapeDtypeStruct((1, N, N), F32),
    )(pick, phase_masks, own, other)


def swapped(x):
    return lax.ppermute(x, CORE, [(0, 1), (1, 0)])


def exchanged(x, axes):
    return lax.all_to_all(x, axes, split_axis=0, concat_axis=0, tiled=True)


def from_everyone(x, axes):
    count = lax.axis_size(axes)
    return exchanged(jnp.broadcast_to(x[None], (count, *x.shape)), axes)


def shards(phase_masks, hg_orders, spot_index):
    plane, core = lax.axis_index("plane"), lax.axis_index(CORE)
    group = core * XY_DEVICES + lax.axis_index(XY)
    pick = jnp.stack([plane, core]).astype(jnp.int32)
    tangent = tangent_call(group.astype(jnp.int32)[None], phase_masks)
    all_planes = from_everyone(tangent, "plane")
    half_own = from_everyone(all_planes, XY)
    half_other = swapped(half_own)
    left, right = block_operators()
    keep, send = main_call(hg_orders, spot_index, pick, half_own, half_other, left, right)
    pair = keep + swapped(send)
    column = jnp.sum(exchanged(pair, XY).astype(F32), axis=0).astype(BF16)
    pieces = jnp.repeat(column, 2, axis=0)
    total = jnp.sum(exchanged(pieces, Z).astype(F32), axis=0).astype(BF16)
    own = from_everyone(total, XY)
    other = swapped(own)
    return finish_call(pick, phase_masks, own, other)


def solution(mesh):
    finer = Mesh(
        mesh.devices.reshape(mesh.shape["plane"], 4, 4, 2, 2),
        ("plane", "mode_0", "mode_1", "mode_2", "mode_3"),
    )
    placed = (P("plane", None, None), P(MODE, None), P(MODE))
    return jax.shard_map(
        shards, mesh=finer, in_specs=placed, out_specs=P("plane", None, None), check_vma=False
    )
```

time: 262 us -> 118 us (0.45)
  loops' own time: 68.2 us -> 0 us
  blocking collectives: 104 us -> 77.6 us
  matrix products: 24.6 us -> 0 us
  local copies, waits for them, and re-layouts: 28 us -> 3.88 us
  Pallas kernels: 0 us -> 21.8 us
  between operations: 19.6 us -> 0.06 us
  other arithmetic: 15.8 us -> 2.49 us
  starting transfers between devices: 0.01 us -> 7.63 us
  waiting for transfers between devices: 0.73 us -> 3.94 us
    another operation x2 -> x0, loops' own time: 68.2 us -> none  [hermite(): lax.fori_loop(1, ORDERS - 1, advance, (lowest, second, chosen))]
    all_to_all x5, blocking collectives: 104 us -> 77.6 us  [exchanged(): return lax.all_to_all(x, axes, split_axis=0, concat_axis=0, tiled=True)]
    dot_general x48 -> x0, matrix products: 24.6 us -> none  [the longest x8 5.82 us: right_product(): jnp.dot(field_sum, right_sum, preferred_element_type=jnp.float32)]
    pallas_call x0 -> x3, Pallas kernels: none -> 21.8 us  [the longest x1 17.5 us: main_call(): pl.pallas_call(main_kernel, name='modes', in_specs=[smem, smem, smem, hbm...]
    sin x1 -> x0, local copies, waits for them, and re-layouts: 16 us -> none  [shards(): sin_masks = jnp.sin(all_masks)]
    ppermute x0 -> x3, starting transfers between devices: none -> 7.63 us  [swapped(): return lax.ppermute(x, CORE, [(0, 1), (1, 0)])]
    reduce_sum x5 -> x2, other arithmetic: 6.39 us -> 0.22 us  [the longest x1 0.2 us: shards(): column = jnp.sum(exchanged(pair, XY).astype(F32), axis=0).astype(BF16)]
    convert_element_type x8 -> x0, other arithmetic: 5.32 us -> none  [the longest x4 1.72 us: apply_mask(): masked_im = (field_re * sin_mask + field_im * cos_mask).astype(jnp.bfloat16)]
  transfers between devices with their start and end apart: 1 -> 3, of which waited for: 0 -> 3; matrix products, arithmetic and copies ran while one was open for 8% -> 1% of each run, Pallas kernels for 0% -> 0%
where the time goes in v1:
time: 118 us; the launch traced here: 117 us
  blocking collectives  77.6 us (66%)
  Pallas kernels  21.8 us (18%)
  starting transfers between devices  7.63 us (6%)
  waiting for transfers between devices  3.94 us (3%)
  local copies, waits for them, and re-layouts  3.88 us (3%)
  other arithmetic  2.49 us (2%)
    all_to_all x5, blocking collectives, exchanged(): return lax.all_to_all(x, axes, split_axis=0, concat_axis=0, tiled=True)  77.6 us
    pallas_call x1, Pallas kernels, main_call(): pl.pallas_call(main_kernel, name='modes', in_specs=[smem, smem, smem, hbm...  17.5 us
    ppermute x3, starting transfers between devices, swapped(): return lax.ppermute(x, CORE, [(0, 1), (1, 0)])  7.63 us
    ppermute x3, waiting for transfers between devices, swapped(): return lax.ppermute(x, CORE, [(0, 1), (1, 0)])  3.94 us
    unnamed x11, local copies, waits for them, and re-layouts  3.02 us
    pallas_call x1, Pallas kernels, finish_call(): pl.pallas_call(finish_kernel, name='finish', in_specs=[smem, vmem, vmem,...  2.73 us
  transfers between devices with their start and end apart: 3, of which 3 were waited for; matrix products, arithmetic and copies ran while one was open for 1% of the time, Pallas kernels for 0%

profile of v1, /device:TPU:1, one launch (start us, length us, event | category | flops | bytes accessed | tf_op | source)
XLA Modules:
  0.0 117.3 jit_solution(11701601655545972885)
XLA Ops:
  0.0 1.5 %tangent.1 = bf16[16,512]{1,0:T(8,128)(2,1)} custom-call(s32[1]{0:T(128)} %bitcast.2.where, f32[1,512,512]{2,1,0:T(8,128)} %phase.3), custom_call_target="tpu_custom_call" | custom-call | tf_op jit(solution)/shard_map/tangent/pallas_call | solution.py:317
  1.5 0.7 broadcast_in_dim.11
  2.2 15.8 %all_to_all.25 = bf16[4,16,512]{2,1,0:T(8,128)(2,1)S(1)} all-to-all(bf16[4,16,512]{2,1,0:T(8,128)(2,1)S(1)} %broadcast_in_dim.11), channel_id=1, replica_groups=mesh['plane'=4,'mode_0'=4,'mode_1'=4,'mode_2'=2,'mode_3'=2] {'plane'}, dimensions={0} | all-to-all | bytes 131072 | tf_op jit(solution)/shard_map/all_to_all | solution.py:361
  18.1 0.1 broadcast_in_dim.12
  18.2 21.5 %all_to_all.26.half_own = bf16[16,4,16,512]{3,2,1,0:T(8,128)(2,1)S(1)} all-to-all(bf16[16,4,16,512]{3,2,1,0:T(8,128)(2,1)S(1)} %broadcast_in_dim.12), channel_id=1, replica_groups=mesh['plane'=4,'mode_0'=4,'mode_1'=4,'mode_2'=2,'mode_3'=2] {'mode_0','m..., dimensions={0} | all-to-all | bytes 2097152 | tf_op jit(solution)/shard_map/all_to_all | solution.py:361
  39.7 0.0 copy-start
  39.7 3.1 %collective-permute-start = (bf16[16,4,16,512]{3,2,1,0:T(8,128)(2,1)S(1)}, bf16[16,4,16,512]{3,2,1,0:T(8,128)(2,1)S(1)}, u32[]{:S(2)}, u32[]{:S(2)}) collective-permute-start(bf16[16,4,16,512]{3,2,1,0:T(8,128)(2,1)S(1)} %all_to_all.26.half_own), channel_id=1, source_target_pairs={{0,1},{1,0},{2,3},{3,2},{4,5},{5,4},{6,7},{7,6},{8,9},{9,8},{10,11... | collective-permute-start | bytes 3145736 | tf_op jit(solution)/shard_map/ppermute | solution.py:357
  42.8 0.0 copy-start.4
  42.8 0.7 copy-done.4
  43.5 0.7 copy.7.orders
  44.2 0.6 pad_add_fusion.pick
  44.8 0.3 collective-permute-done.half_other
  45.1 0.0 copy-done
  45.1 0.0 copy-start.1
  45.1 1.0 copy-done.1
  46.1 17.5 %modes.1 = (bf16[16,4,16,512]{3,2,1,0:T(8,128)(2,1)}, bf16[16,4,16,512]{3,2,1,0:T(8,128)(2,1)}) custom-call(s32[4,2]{1,0:T(4,128)} %copy.7.orders, s32[4]{0:T(128)} %spots.1, s32[2]{0:T(128)} %pad_add_fusion.pick, bf16[16,4,16,512]{3,2,1,0:T(8,128)(2,1)} %copy-done, bf16[16,4,16,512]{3,2,1,0:T(8,128)(2,1)} %copy-done.1, bf16[4,256,256]{2,1,0:T(8,128)(2,1)} %constant.34.left, ...), custom_call_target="tpu_custom_call" | custom-call | tf_op jit(solution)/shard_map/modes/pallas_call | solution.py:289
  63.6 0.5 collective-permute-start.1
  64.0 2.5 %collective-permute-done.1 = bf16[16,4,16,512]{3,2,1,0:T(8,128)(2,1)S(1)} collective-permute-done((bf16[16,4,16,512]{3,2,1,0:T(8,128)(2,1)}, bf16[16,4,16,512]{3,2,1,0:T(8,128)(2,1)S(1)}, u32[]{:S(2)}, u32[]{:S(2)}) %collective-permute-start.1) | collective-permute-done | bytes 1048608 | tf_op jit(solution)/shard_map/ppermute | solution.py:357
  66.5 1.6 %add.11 = bf16[16,4,16,512]{3,2,1,0:T(8,128)(2,1)S(1)} add(bf16[16,4,16,512]{3,2,1,0:T(8,128)(2,1)} %get-tuple-element.7, bf16[16,4,16,512]{3,2,1,0:T(8,128)(2,1)S(1)} %collective-permute-done.1) | non-fusion elementwise | flops 524288 | bytes 3145728 | tf_op jit(solution)/shard_map/add | solution.py:379
  68.2 19.1 %all_to_all.27 = bf16[16,4,16,512]{3,2,1,0:T(8,128)(2,1)S(1)} all-to-all(bf16[16,4,16,512]{3,2,1,0:T(8,128)(2,1)S(1)} %add.11), channel_id=1, replica_groups=mesh['plane'=4,'mode_0'=4,'mode_1'=4,'mode_2'=2,'mode_3'=2] {'mode_0','m..., dimensions={0} | all-to-all | bytes 2097152 | tf_op jit(solution)/shard_map/all_to_all | solution.py:361
  87.2 0.2 reduce_sum.24
  87.5 10.4 %all_to_all.28 = bf16[8,16,512]{2,1,0:T(8,128)(2,1)S(1)} all-to-all(bf16[8,16,512]{2,1,0:T(8,128)(2,1)S(1)} %bitcast.4), channel_id=1, replica_groups=mesh['plane'=4,'mode_0'=4,'mode_1'=4,'mode_2'=2,'mode_3'=2] {'plane','mo..., dimensions={0} | all-to-all | bytes 262144 | tf_op jit(solution)/shard_map/all_to_all | solution.py:361
  97.9 10.8 %all_to_all.29.own = bf16[16,16,512]{2,1,0:T(8,128)(2,1)S(1)} all-to-all(bf16[16,16,512]{2,1,0:T(8,128)(2,1)S(1)} %broadcast_in_dim.28), channel_id=1, replica_groups=mesh['plane'=4,'mode_0'=4,'mode_1'=4,'mode_2'=2,'mode_3'=2] {'mode_0','m..., dimensions={0} | all-to-all | bytes 524288 | tf_op jit(solution)/shard_map/all_to_all | solution.py:361
  108.7 0.0 copy-start.2
  108.7 4.0 %collective-permute-start.2 = (bf16[16,16,512]{2,1,0:T(8,128)(2,1)S(1)}, bf16[16,16,512]{2,1,0:T(8,128)(2,1)S(1)}, u32[]{:S(2)}, u32[]{:S(2)}) collective-permute-start(bf16[16,16,512]{2,1,0:T(8,128)(2,1)S(1)} %all_to_all.29.own), channel_id=1, source_target_pairs={{0,1},{1,0},{2,3},{3,2},{4,5},{5,4},{6,7},{7,6},{8,9},{9,8},{10,11... | collective-permute-start | bytes 786440 | tf_op jit(solution)/shard_map/ppermute | solution.py:357
  112.8 1.2 collective-permute-done.2.other
  113.9 0.0 copy-done.2
  113.9 0.0 copy-start.3
  113.9 0.7 copy-done.3
  114.6 2.7 %finish.1 = f32[1,512,512]{2,1,0:T(8,128)} custom-call(s32[2]{0:T(128)} %pad_add_fusion.pick, f32[1,512,512]{2,1,0:T(8,128)} %phase.3, bf16[16,16,512]{2,1,0:T(8,128)(2,1)} %copy-done.2, bf16[16,16,512]{2,1,0:T(8,128)(2,1)} %copy-done.3), custom_call_target="tpu_custom_call" | custom-call | tf_op jit(solution)/shard_map/finish/pallas_call | solution.py:347
  (3 shorter events, 0.1 us)
Async XLA Ops:
  39.7 5.4 %copy-start = (bf16[16,4,16,512]{3,2,1,0:T(8,128)(2,1)}, bf16[16,4,16,512]{3,2,1,0:T(8,128)(2,1)S(1)}, u32[]{:S(2)}) copy-start(bf16[16,4,16,512]{3,2,1,0:T(8,128)(2,1)S(1)} %all_to_all.26.half_own) | copy-start | bytes 3145732
  39.7 5.4 %collective-permute-start = (bf16[16,4,16,512]{3,2,1,0:T(8,128)(2,1)S(1)}, bf16[16,4,16,512]{3,2,1,0:T(8,128)(2,1)S(1)}, u32[]{:S(2)}, u32[]{:S(2)}) collective-permute-start(bf16[16,4,16,512]{3,2,1,0:T(8,128)(2,1)S(1)} %all_to_all.26.half_own), channel_id=1, source_target_pairs={{0,1},{1,0},{2,3},{3,2},{4,5},{5,4},{6,7},{7,6},{8,9},{9,8},{10,11... | collective-permute-start | bytes 3145736 | tf_op jit(solution)/shard_map/ppermute | solution.py:357
  42.8 0.7 copy-start.4
  45.1 1.0 copy-start.1
  63.6 3.0 %collective-permute-start.1 = (bf16[16,4,16,512]{3,2,1,0:T(8,128)(2,1)}, bf16[16,4,16,512]{3,2,1,0:T(8,128)(2,1)S(1)}, u32[]{:S(2)}, u32[]{:S(2)}) collective-permute-start(bf16[16,4,16,512]{3,2,1,0:T(8,128)(2,1)} %get-tuple-element.8), channel_id=1, source_target_pairs={{0,1},{1,0},{2,3},{3,2},{4,5},{5,4},{6,7},{7,6},{8,9},{9,8},{10,11... | collective-permute-start | bytes 3145736 | tf_op jit(solution)/shard_map/ppermute | solution.py:357
  108.7 5.2 %copy-start.2 = (bf16[16,16,512]{2,1,0:T(8,128)(2,1)}, bf16[16,16,512]{2,1,0:T(8,128)(2,1)S(1)}, u32[]{:S(2)}) copy-start(bf16[16,16,512]{2,1,0:T(8,128)(2,1)S(1)} %all_to_all.29.own) | copy-start | bytes 786436
  108.7 5.2 %collective-permute-start.2 = (bf16[16,16,512]{2,1,0:T(8,128)(2,1)S(1)}, bf16[16,16,512]{2,1,0:T(8,128)(2,1)S(1)}, u32[]{:S(2)}, u32[]{:S(2)}) collective-permute-start(bf16[16,16,512]{2,1,0:T(8,128)(2,1)S(1)} %all_to_all.29.own), channel_id=1, source_target_pairs={{0,1},{1,0},{2,3},{3,2},{4,5},{5,4},{6,7},{7,6},{8,9},{9,8},{10,11... | collective-permute-start | bytes 786440 | tf_op jit(solution)/shard_map/ppermute | solution.py:357
  113.9 0.7 copy-start.3

commit v2 on v1

v2 whole, which is shorter than its diff:
```python
import functools
import math

import jax
import jax.numpy as jnp
import numpy as np
from jax import lax
from jax.experimental import pallas as pl
from jax.experimental.pallas import tpu as pltpu
from jax.sharding import Mesh
from jax.sharding import PartitionSpec as P

ORDERS = 45
SPOT_SIDE = 32
MODE = ("mode_0", "mode_1", "mode_2", "mode_3")
XY = ("mode_0", "mode_1")
CHIPS = ("mode_0", "mode_1", "mode_2")
CORE = "mode_3"
XY_DEVICES = 16
PLANES = 4
N = 512
B = 128
STRIP = 16
HALF_STRIPS = N // STRIP // 2
CHIRP_RATE = math.pi / 48.0 * (math.pi / 48.0)
AMPLITUDE = 12.0
EPSILON = 1e-06
F32 = jnp.float32
BF16 = jnp.bfloat16
SMEM = pl.BlockSpec(memory_space=pltpu.SMEM)
VMEM = pl.BlockSpec(memory_space=pltpu.VMEM)
ANY = pl.BlockSpec(memory_space=pl.ANY)


def vmem_limit(mib):
    return pltpu.CompilerParams(vmem_limit_bytes=mib << 20)


def block_operators():
    f = np.arange(N)
    s = (f + N // 2) % N - N // 2
    chirp = np.exp(-1j * CHIRP_RATE * s.astype(np.float64) ** 2)
    phase = np.exp(2j * np.pi * ((f[:, None] * f[None, :]) % N) / N)
    kernel = (phase * chirp[None, :]).sum(axis=1) / N
    offset = np.arange(B)[:, None] - np.arange(B)[None, :]
    left, right = [], []
    for k in range(4):
        block = sum((-1j) ** (k * m) * kernel[(offset + B * m) % N] for m in range(4)) / 4.0
        real = np.block([[block.real, -block.imag], [block.imag, block.real]])
        left.append(real)
        right.append(real.T)
    to = lambda x: jnp.asarray(np.stack(x).astype(np.float32)).astype(BF16)
    return to(left), to(right)


def add(x, y):
    return (x[0] + y[0], x[1] + y[1])


def sub(x, y):
    return (x[0] - y[0], x[1] - y[1])


def turned(x, y):
    return (x[0] - y[1], x[1] + y[0])


def turned_back(x, y):
    return (x[0] + y[1], x[1] - y[0])


def dft4(x):
    a, b, c, d = add(x[0], x[2]), sub(x[0], x[2]), add(x[1], x[3]), sub(x[1], x[3])
    return [add(a, c), turned_back(b, d), sub(a, c), turned(b, d)]


def idft4(x):
    a, b, c, d = add(x[0], x[2]), sub(x[0], x[2]), add(x[1], x[3]), sub(x[1], x[3])
    return [add(a, c), turned(b, d), sub(a, c), turned_back(b, d)]


def both_ways(grid, transform):
    grid = [transform(row) for row in grid]
    cols = [transform([grid[k][l] for k in range(4)]) for l in range(4)]
    return [[cols[l][k] for l in range(4)] for k in range(4)]


def mul(x, y):
    return (x[0] * y[0] - x[1] * y[1], x[0] * y[1] + x[1] * y[0])


def dot(a, b):
    return jnp.dot(a, b, preferred_element_type=F32)


def lanes(l):
    return slice(l * B, (l + 1) * B)


def half_angle_tangent(phase):
    x = 0.5 * phase
    y = x * x
    sine, cosine = 0.0, 0.0
    for n in reversed(range(7)):
        sine = sine * y + (-1) ** n / math.factorial(2 * n + 1)
        cosine = cosine * y + (-1) ** n / math.factorial(2 * n)
    return x * sine / cosine


def hermite_tables(psi):
    t = (lax.broadcasted_iota(jnp.int32, (8, N), 1).astype(F32) - (N - 1) / 2.0) / (N / 48.0)
    previous = math.pow(math.pi, -0.25) * jnp.exp(-0.5 * t * t)
    current = math.sqrt(2.0) * t * previous
    psi[0] = previous
    psi[1] = current
    for n in range(1, ORDERS - 1):
        higher = math.sqrt(2.0 / (n + 1.0)) * t * current - math.sqrt(n / (n + 1.0)) * previous
        psi[n + 1] = higher
        previous, current = current, higher


def spot_profile(index, shape, dim):
    coords = lax.broadcasted_iota(jnp.int32, shape, dim).astype(F32) - (N - 1) / 2.0
    centre = index.astype(F32) - (SPOT_SIDE - 1) / 2.0
    offset = (coords - (N / 40.0) * centre) / (N / 120.0)
    return jnp.exp(-offset * offset)


def split(x):
    high = x.astype(BF16)
    return high, (x - high.astype(F32)).astype(BF16)


def main_kernel(
    plane_id, core_id, orders, spots, tan_own, half_own, half_other, left, right, keep, send,
    psi, source_x, far_x, x_ref, v_ref, y_ref, g_ref, mask_ref, tan_ref, grad, sems,
):
    mode, core = plane_id[0], core_id[0]
    arrivals = [pltpu.make_async_copy(tan_own, tan_ref.at[0], sems.at[0])]
    for j in range(1, PLANES):
        for n, (half, at) in enumerate(((half_own, core), (half_other, 1 - core))):
            arrivals.append(
                pltpu.make_async_copy(half.at[:, j - 1], tan_ref.at[j, at], sems.at[2 * j + n - 1])
            )
    for copy in arrivals:
        copy.start()
    hermite_tables(psi)
    source_y = psi[orders[1, mode]]
    row = AMPLITUDE * psi[orders[0, mode]][0:1]
    for k in range(4):
        source_x[k * B : (k + 1) * B, :] = jnp.broadcast_to(row[:, lanes(k)], (B, B)).T

    spot = spots[mode]
    down = spot_profile(spot // SPOT_SIDE, (N, B), 0)
    zero = jnp.zeros((B, B), F32)
    spread = dft4([(down[k * B : (k + 1) * B], zero) for k in range(4)])
    moved = []
    for k in range(4):
        high, low = split(jnp.concatenate(spread[k], axis=0))
        both = dot(left[k], jnp.concatenate([high, low], axis=1))
        total = both[:, :B] + both[:, B:]
        moved.append((total[:B], total[B:]))
    for k, part in enumerate(idft4(moved)):
        far_x[0, k * B : (k + 1) * B, :] = part[0]
        far_x[1, k * B : (k + 1) * B, :] = part[1]
    along = spot_profile(spot % SPOT_SIDE, (8, N), 1)
    zero = jnp.zeros((8, B), F32)
    spread = dft4([(along[:, lanes(l)], zero) for l in range(4)])
    moved = []
    for l in range(4):
        high, low = split(jnp.concatenate(spread[l], axis=1))
        both = dot(jnp.concatenate([high, low], axis=0), right[l])
        total = both[:8] + both[8:]
        moved.append((total[:, :B], total[:, B:]))
    far_y = idft4(moved)

    def rows_of(k, s):
        return pl.ds(k * B + s * STRIP, STRIP)

    def decode(plane, s):
        slot = mode ^ plane
        for k in range(4):
            t = tan_ref[slot, k // 2, (k % 2) * (B // STRIP) + s].astype(F32)
            twice = 2.0 / (1.0 + t * t)
            mask_ref[plane, 0, rows_of(k, s), :] = (twice - 1.0).astype(BF16)
            mask_ref[plane, 1, rows_of(k, s), :] = (twice * t).astype(BF16)

    def mask_at(plane, k, l, s):
        at = mask_ref.at[plane]
        return (at[0, rows_of(k, s), lanes(l)], at[1, rows_of(k, s), lanes(l)])

    def spread_out(grid, s):
        grid = both_ways(grid, dft4)
        for k in range(4):
            for l in range(4):
                x_ref[k, pl.ds(s * STRIP, STRIP), lanes(l)] = grid[k][l][0]
                x_ref[k, pl.ds(B + s * STRIP, STRIP), lanes(l)] = grid[k][l][1]

    def gathered_up(s):
        grid = [
            [(y_ref[l, rows_of(k, s), 0:B], y_ref[l, rows_of(k, s), B : 2 * B]) for l in range(4)]
            for k in range(4)
        ]
        return both_ways(grid, idft4)

    def operate():
        for k in range(4):
            z = dot(left[k], x_ref[k]).astype(BF16)
            for l in range(4):
                v_ref[l, k * B : (k + 1) * B, 0:B] = z[:B, lanes(l)]
                v_ref[l, k * B : (k + 1) * B, B : 2 * B] = z[B:, lanes(l)]
        for l in range(4):
            y_ref[l] = dot(v_ref[l], right[l]).astype(BF16)

    def masked(plane, field, k, l, s):
        g = mul(field, mask_at(plane, k, l, s))
        g_ref[plane, 0, rows_of(k, s), lanes(l)] = g[0]
        g_ref[plane, 1, rows_of(k, s), lanes(l)] = g[1]
        return g

    def first_strip(s, carry):
        decode(0, s)

        def at(k, l):
            field = (source_x[rows_of(k, s), :] * source_y[0:1, lanes(l)]).astype(BF16)
            mask = mask_at(0, k, l, s)
            g = (field * mask[0], field * mask[1])
            g_ref[0, 0, rows_of(k, s), lanes(l)] = g[0]
            g_ref[0, 1, rows_of(k, s), lanes(l)] = g[1]
            return g

        spread_out([[at(k, l) for l in range(4)] for k in range(4)], s)
        return carry

    def forward_strip(plane, s, carry):
        decode(plane, s)
        field = gathered_up(s)
        spread_out([[masked(plane, field[k][l], k, l, s) for l in range(4)] for k in range(4)], s)
        return carry

    def last_strip(s, carry):
        decode(PLANES - 1, s)
        field = gathered_up(s)
        carry = list(carry)
        for k in range(4):
            a = (far_x[0, rows_of(k, s), :], far_x[1, rows_of(k, s), :])
            for l in range(4):
                g = masked(PLANES - 1, field[k][l], k, l, s)
                carry[l] = add(carry[l], mul((g[0].astype(F32), g[1].astype(F32)), a))
        return tuple(carry)

    def returned(plane, back, k, l, s):
        g = (g_ref[plane, 0, rows_of(k, s), lanes(l)], g_ref[plane, 1, rows_of(k, s), lanes(l)])
        piece = 2 * ((k % 2) * (B // STRIP) + s) + l // 2
        grad[k // 2, piece, mode ^ plane, :, lanes(l % 2)] = back[0] * g[1] + back[1] * g[0]
        return mul(back, mask_at(plane, k, l, s)) if plane else None

    strips = B // STRIP
    for copy in arrivals:
        copy.wait()
    lax.fori_loop(0, strips, first_strip, 0)
    for plane in range(1, PLANES - 1):
        operate()
        lax.fori_loop(0, strips, functools.partial(forward_strip, plane), 0)
    operate()
    nothing = jnp.zeros((STRIP, B), F32)
    sums = lax.fori_loop(0, strips, last_strip, tuple((nothing, nothing) for _ in range(4)))
    total = [mul((s[0][:8] + s[0][8:], s[1][:8] + s[1][8:]), y) for s, y in zip(sums, far_y)]
    coupling_re = jnp.sum(sum(t[0] for t in total))
    coupling_im = jnp.sum(sum(t[1] for t in total))
    back_y = [
        (
            (coupling_re * y[0] + coupling_im * y[1])[0:1],
            (coupling_re * y[1] - coupling_im * y[0])[0:1],
        )
        for y in far_y
    ]

    def turn_strip(s, carry):
        def at(k, l):
            a = (far_x[0, rows_of(k, s), :], far_x[1, rows_of(k, s), :])
            back = mul(a, back_y[l])
            return returned(PLANES - 1, (back[0].astype(BF16), back[1].astype(BF16)), k, l, s)

        spread_out([[at(k, l) for l in range(4)] for k in range(4)], s)
        return carry

    def backward_strip(plane, s, carry):
        back = gathered_up(s)
        reply = [[returned(plane, back[k][l], k, l, s) for l in range(4)] for k in range(4)]
        if plane:
            spread_out(reply, s)
        return carry

    lax.fori_loop(0, strips, turn_strip, 0)
    for plane in reversed(range(PLANES - 1)):
        operate()
        lax.fori_loop(0, strips, functools.partial(backward_strip, plane), 0)
    departures = [
        pltpu.make_async_copy(grad.at[1 - core], send, sems.at[0]),
        pltpu.make_async_copy(grad.at[core], keep, sems.at[1]),
    ]
    for copy in departures:
        copy.start()
    for copy in departures:
        copy.wait()


def main_call(plane_id, core_id, orders, spots, tan_own, half_own, half_other, left, right):
    pieces = (2 * HALF_STRIPS, PLANES, STRIP, N // 2)
    return pl.pallas_call(
        main_kernel,
        name="modes",
        in_specs=[SMEM, SMEM, SMEM, SMEM, ANY, ANY, ANY, VMEM, VMEM],
        out_specs=[ANY, ANY],
        out_shape=[jax.ShapeDtypeStruct(pieces, BF16)] * 2,
        scratch_shapes=[
            pltpu.VMEM((ORDERS, 8, N), F32),
            pltpu.VMEM((N, B), F32),
            pltpu.VMEM((2, N, B), F32),
            pltpu.VMEM((4, 2 * B, N), BF16),
            pltpu.VMEM((4, N, 2 * B), BF16),
            pltpu.VMEM((4, N, 2 * B), BF16),
            pltpu.VMEM((PLANES, 2, N, N), BF16),
            pltpu.VMEM((PLANES, 2, N, N), BF16),
            pltpu.VMEM((PLANES, 2, HALF_STRIPS, STRIP, N), BF16),
            pltpu.VMEM((2, *pieces), BF16),
            pltpu.SemaphoreType.DMA((7,)),
        ],
        compiler_params=vmem_limit(26),
    )(plane_id, core_id, orders, spots, tan_own, half_own, half_other, left, right)


def tangent_kernel(where, phase, out, rows, sem):
    copy = pltpu.make_async_copy(phase.at[0, pl.ds(where[0] * STRIP, STRIP)], rows, sem)
    copy.start()
    copy.wait()
    out[...] = half_angle_tangent(rows[...]).astype(BF16)


def tangent_call(where, phase_masks):
    return pl.pallas_call(
        tangent_kernel,
        name="tangent",
        in_specs=[SMEM, pl.BlockSpec(memory_space=pltpu.HBM)],
        out_specs=VMEM,
        out_shape=jax.ShapeDtypeStruct((STRIP, N), BF16),
        scratch_shapes=[pltpu.VMEM((STRIP, N), F32), pltpu.SemaphoreType.DMA],
        compiler_params=vmem_limit(4),
    )(where, phase_masks)


def own_tangent_kernel(phase, out):
    def strip(i, carry):
        x = phase[0, pl.ds(i * STRIP, STRIP), :]
        out[i // HALF_STRIPS, i % HALF_STRIPS] = half_angle_tangent(x).astype(BF16)
        return carry

    lax.fori_loop(0, N // STRIP, strip, 0)


def own_tangent_call(phase_masks):
    return pl.pallas_call(
        own_tangent_kernel,
        name="own_tangent",
        in_specs=[VMEM],
        out_specs=VMEM,
        out_shape=jax.ShapeDtypeStruct((2, HALF_STRIPS, STRIP, N), BF16),
        compiler_params=vmem_limit(6),
    )(phase_masks)


def finish_kernel(core_id, phase, own, other, out):
    squares = jnp.zeros((STRIP, N // 2), F32)
    for piece in range(2 * HALF_STRIPS):
        for part in (own, other):
            x = part[piece].astype(F32)
            squares += x * x
    mean = 4.0 * jnp.sum(squares, keepdims=True) / (N * N)
    scale = -2.0 * lax.rsqrt(mean + EPSILON)
    core = core_id[0]
    for part, half in ((own, core), (other, 1 - core)):
        for piece in range(2 * HALF_STRIPS):
            rows = pl.ds(half * (N // 2) + (piece // 2) * STRIP, STRIP)
            cols = slice((piece % 2) * (N // 2), (piece % 2 + 1) * (N // 2))
            out[0, rows, cols] = phase[0, rows, cols] + part[piece].astype(F32) * scale


def finish_call(core_id, phase_masks, own, other):
    return pl.pallas_call(
        finish_kernel,
        name="finish",
        in_specs=[SMEM, VMEM, VMEM, VMEM],
        out_specs=VMEM,
        out_shape=jax.ShapeDtypeStruct((1, N, N), F32),
        compiler_params=vmem_limit(8),
    )(core_id, phase_masks, own, other)


def swapped(x):
    return lax.ppermute(x, CORE, [(0, 1), (1, 0)])


def from_plane(x, step):
    return lax.ppermute(x, "plane", [(p, p ^ step) for p in range(PLANES)])


def exchanged(x, axes):
    return lax.all_to_all(x, axes, split_axis=0, concat_axis=0, tiled=True)


def from_everyone(x, axes):
    count = lax.axis_size(axes)
    return exchanged(jnp.broadcast_to(x[None], (count, *x.shape)), axes)


def shards(phase_masks, hg_orders, spot_index):
    core = lax.axis_index(CORE).astype(jnp.int32)
    plane_id, core_id = lax.axis_index("plane").astype(jnp.int32)[None], core[None]
    group = core * XY_DEVICES + lax.axis_index(XY).astype(jnp.int32)
    tangent = tangent_call(group[None], phase_masks)
    tan_own = own_tangent_call(phase_masks)
    near = from_plane(tangent, 1)
    far = from_plane(jnp.stack([tangent, near]), 2)
    half_own = from_everyone(jnp.concatenate([near[None], far]), XY)
    half_other = swapped(half_own)
    left, right = block_operators()
    keep, send = main_call(
        plane_id, core_id, hg_orders.T, spot_index, tan_own, half_own, half_other, left, right
    )
    pair = keep + swapped(send)
    column = jnp.sum(exchanged(pair, CHIPS).astype(F32), axis=0).astype(BF16)
    two = column[:2] + from_plane(column[2:], 2)
    total = two[0] + from_plane(two[1], 1)
    own = from_everyone(total, CHIPS)
    other = swapped(own)
    return finish_call(core_id, phase_masks, own, other)


def solution(mesh):
    finer = Mesh(
        mesh.devices.reshape(mesh.shape["plane"], 4, 4, 2, 2),
        ("plane", "mode_0", "mode_1", "mode_2", "mode_3"),
    )
    placed = (P("plane", None, None), P(MODE, None), P(MODE))
    return jax.shard_map(
        shards, mesh=finer, in_specs=placed, out_specs=P("plane", None, None), check_vma=False
    )
```

time: 118 us -> 108 us (0.915)
  blocking collectives: 77.6 us -> 49.6 us
  starting transfers between devices: 7.63 us -> 28.2 us
  Pallas kernels: 21.8 us -> 16.3 us
  waiting for transfers between devices: 3.94 us -> 8.66 us
  other arithmetic: 2.49 us -> 0.55 us
    all_to_all x5 -> x3, blocking collectives: 77.6 us -> 49.6 us  [exchanged(): return lax.all_to_all(x, axes, split_axis=0, concat_axis=0, tiled=True)]
    ppermute x0 -> x4, starting transfers between devices: none -> 18.2 us  [from_plane(): return lax.ppermute(x, 'plane', [(p, p ^ step) for p in range(PLANES)])]
    pallas_call x3 -> x4, Pallas kernels: 21.8 us -> 16.3 us  [the longest x1 13.5 us: main_call(): pl.pallas_call(main_kernel, name='modes', in_specs=[SMEM, SMEM, SMEM, SME...]
    ppermute x0 -> x4, waiting for transfers between devices: none -> 4.74 us  [from_plane(): return lax.ppermute(x, 'plane', [(p, p ^ step) for p in range(PLANES)])]
    ppermute x3, starting transfers between devices: 7.63 us -> 10 us  [swapped(): return lax.ppermute(x, CORE, [(0, 1), (1, 0)])]
    add x1, other arithmetic: 1.63 us -> 0.37 us  [shards(): pair = keep + swapped(send)]
    unnamed x11 -> x12, local copies, waits for them, and re-layouts: 3.02 us -> 3.99 us
  transfers between devices with their start and end apart: 3 -> 7, of which waited for: 3 -> 7; matrix products, arithmetic and copies ran while one was open for 1% -> 0% of each run, Pallas kernels for 0% -> 1%
where the time goes in v2:
time: 108 us; the launch traced here: 107 us
  blocking collectives  49.6 us (46%)
  starting transfers between devices  28.2 us (26%)
  Pallas kernels  16.3 us (15%)
  waiting for transfers between devices  8.66 us (8%)
  local copies, waits for them, and re-layouts  4.1 us (4%)
    all_to_all x3, blocking collectives, exchanged(): return lax.all_to_all(x, axes, split_axis=0, concat_axis=0, tiled=True)  49.6 us
    ppermute x4, starting transfers between devices, from_plane(): return lax.ppermute(x, 'plane', [(p, p ^ step) for p in range(PLANES)])  18.2 us
    pallas_call x1, Pallas kernels, main_call(): pl.pallas_call(main_kernel, name='modes', in_specs=[SMEM, SMEM, SMEM, SME...  13.5 us
    ppermute x3, starting transfers between devices, swapped(): return lax.ppermute(x, CORE, [(0, 1), (1, 0)])  10 us
    ppermute x4, waiting for transfers between devices, from_plane(): return lax.ppermute(x, 'plane', [(p, p ^ step) for p in range(PLANES)])  4.74 us
    unnamed x12, local copies, waits for them, and re-layouts  3.99 us
    ppermute x3, waiting for transfers between devices, swapped(): return lax.ppermute(x, CORE, [(0, 1), (1, 0)])  3.92 us
  transfers between devices with their start and end apart: 7, of which 7 were waited for; matrix products, arithmetic and copies ran while one was open for 0% of the time, Pallas kernels for 1%

profile of v2, /device:TPU:1, one launch (start us, length us, event | category | flops | bytes accessed | tf_op | source)
XLA Modules:
  0.0 107.5 jit_solution(14109216359411858351)
XLA Ops:
  0.0 0.0 copy-start
  0.0 1.2 %copy-done = f32[1,512,512]{2,1,0:T(8,128)S(1)} copy-done((f32[1,512,512]{2,1,0:T(8,128)S(1)}, f32[1,512,512]{2,1,0:T(8,128)}, u32[]{:S(2)}) %copy-start) | copy-done | bytes 1048600
  1.2 0.1 tangent.1
  1.3 3.9 %collective-permute-start = (bf16[16,512]{1,0:T(8,128)(2,1)S(1)}, bf16[16,512]{1,0:T(8,128)(2,1)S(1)}, u32[]{:S(2)}, u32[]{:S(2)}) collective-permute-start(bf16[16,512]{1,0:T(8,128)(2,1)S(1)} %tangent.1), channel_id=1, source_target_pairs={{0,64},{64,0},{128,192},{192,128},{1,65},{65,1},{129,193},{193,129... | collective-permute-start | bytes 49160 | tf_op jit(solution)/shard_map/ppermute | solution.py:405
  5.2 1.1 %collective-permute-done = bf16[16,512]{1,0:T(8,128)(2,1)S(1)} collective-permute-done((bf16[16,512]{1,0:T(8,128)(2,1)S(1)}, bf16[16,512]{1,0:T(8,128)(2,1)S(1)}, u32[]{:S(2)}, u32[]{:S(2)}) %collective-permute-start) | collective-permute-done | bytes 16416 | tf_op jit(solution)/shard_map/ppermute | solution.py:405
  6.3 6.3 %collective-permute-start.1 = (bf16[2,16,512]{2,1,0:T(8,128)(2,1)S(1)}, bf16[2,16,512]{2,1,0:T(8,128)(2,1)S(1)}, u32[]{:S(2)}, u32[]{:S(2)}) collective-permute-start(bf16[2,16,512]{2,1,0:T(8,128)(2,1)S(1)} %pad_maximum_fusion.1), channel_id=1, source_target_pairs={{0,128},{64,192},{128,0},{192,64},{1,129},{65,193},{129,1},{193,65... | collective-permute-start | bytes 98312 | tf_op jit(solution)/shard_map/ppermute | solution.py:405
  12.6 1.3 %collective-permute-done.1 = bf16[2,16,512]{2,1,0:T(8,128)(2,1)S(1)} collective-permute-done((bf16[2,16,512]{2,1,0:T(8,128)(2,1)S(1)}, bf16[2,16,512]{2,1,0:T(8,128)(2,1)S(1)}, u32[]{:S(2)}, u32[]{:S(2)}) %collective-permute-start.1) | collective-permute-done | bytes 32800 | tf_op jit(solution)/shard_map/ppermute | solution.py:405
  13.9 0.0 copy-start.1
  13.9 0.1 broadcast_in_dim.28
  14.0 17.4 %all_to_all.15.half_own = bf16[16,3,16,512]{3,2,1,0:T(8,128)(2,1)S(1)} all-to-all(bf16[16,3,16,512]{3,2,1,0:T(8,128)(2,1)S(1)} %broadcast_in_dim.28), channel_id=1, replica_groups=mesh['plane'=4,'mode_0'=4,'mode_1'=4,'mode_2'=2,'mode_3'=2] {'mode_0','m..., dimensions={0} | all-to-all | bytes 1572864 | tf_op jit(solution)/shard_map/all_to_all | solution.py:409
  31.4 4.4 %collective-permute-start.2 = (bf16[16,3,16,512]{3,2,1,0:T(8,128)(2,1)S(1)}, bf16[16,3,16,512]{3,2,1,0:T(8,128)(2,1)S(1)}, u32[]{:S(2)}, u32[]{:S(2)}) collective-permute-start(bf16[16,3,16,512]{3,2,1,0:T(8,128)(2,1)S(1)} %all_to_all.15.half_own), channel_id=1, source_target_pairs={{0,1},{1,0},{2,3},{3,2},{4,5},{5,4},{6,7},{7,6},{8,9},{9,8},{10,11... | collective-permute-start | bytes 2359304 | tf_op jit(solution)/shard_map/ppermute | solution.py:401
  35.8 0.0 copy-done.1
  35.8 1.4 %own_tangent.1.tan_own = bf16[2,16,16,512]{3,2,1,0:T(8,128)(2,1)S(1)} custom-call(f32[1,512,512]{2,1,0:T(8,128)S(1)} %copy-done.1), custom_call_target="tpu_custom_call" | custom-call | tf_op jit(solution)/shard_map/own_tangent/pallas_call | solution.py:363
  37.2 0.5 collective-permute-done.2.half_other
  37.7 0.0 copy-start.4
  37.7 0.0 copy-start.5
  37.7 0.7 copy-done.4
  38.4 0.0 copy-done.5
  38.4 0.0 copy-start.2
  38.4 1.0 copy-done.2
  39.4 0.0 copy-start.3
  39.4 1.0 copy-done.3
  40.5 13.5 %modes.1 = (bf16[32,4,16,256]{3,2,1,0:T(8,128)(2,1)S(1)}, bf16[32,4,16,256]{3,2,1,0:T(8,128)(2,1)S(1)}) custom-call(s32[1]{0:T(128)} %bitcast.1.plane_id, s32[1]{0:T(128)} %bitcast.core_id, s32[2,4]{1,0:T(2,128)S(1)} %bitcast.13, s32[4]{0:T(128)S(1)} %copy-done.5, bf16[2,16,16,512]{3,2,1,0:T(8,128)(2,1)S(1)} %own_tangent.1.tan_own, ...), custom_call_target="tpu_custom_call" | custom-call | tf_op jit(solution)/shard_map/modes/pallas_call | solution.py:311
  53.9 0.5 collective-permute-start.3
  54.4 2.3 %collective-permute-done.3 = bf16[32,4,16,256]{3,2,1,0:T(8,128)(2,1)S(1)} collective-permute-done((bf16[32,4,16,256]{3,2,1,0:T(8,128)(2,1)S(1)}, bf16[32,4,16,256]{3,2,1,0:T(8,128)(2,1)S(1)}, u32[]{:S(2)}, u32[]{:S(2)}) %collective-permute-start.3) | collective-permute-done | bytes 1048608 | tf_op jit(solution)/shard_map/ppermute | solution.py:401
  56.7 0.4 add.17
  57.1 20.9 %all_to_all.16 = bf16[32,4,16,256]{3,2,1,0:T(8,128)(2,1)S(1)} all-to-all(bf16[32,4,16,256]{3,2,1,0:T(8,128)(2,1)S(1)} %add.17), channel_id=1, replica_groups=mesh['plane'=4,'mode_0'=4,'mode_1'=4,'mode_2'=2,'mode_3'=2] {'mode_0','m..., dimensions={0} | all-to-all | bytes 2097152 | tf_op jit(solution)/shard_map/all_to_all | solution.py:409
  78.0 0.2 reduce_sum.12
  78.2 5.5 %collective-permute-start.4 = (bf16[2,16,256]{2,1,0:T(8,128)(2,1)S(1)}, bf16[2,16,256]{2,1,0:T(8,128)(2,1)S(1)}, u32[]{:S(2)}, u32[]{:S(2)}) collective-permute-start(bf16[2,16,256]{2,1,0:T(8,128)(2,1)S(1)} %slice.17), channel_id=1, source_target_pairs={{0,128},{64,192},{128,0},{192,64},{1,129},{65,193},{129,1},{193,65... | collective-permute-start | bytes 49160 | tf_op jit(solution)/shard_map/ppermute | solution.py:405
  83.6 1.1 %collective-permute-done.4 = bf16[2,16,256]{2,1,0:T(8,128)(2,1)S(1)} collective-permute-done((bf16[2,16,256]{2,1,0:T(8,128)(2,1)S(1)}, bf16[2,16,256]{2,1,0:T(8,128)(2,1)S(1)}, u32[]{:S(2)}, u32[]{:S(2)}) %collective-permute-start.4) | collective-permute-done | bytes 16416 | tf_op jit(solution)/shard_map/ppermute | solution.py:405
  84.8 2.5 %collective-permute-start.5 = (bf16[16,256]{1,0:T(8,128)(2,1)S(1)}, bf16[16,256]{1,0:T(8,128)(2,1)S(1)}, u32[]{:S(2)}, u32[]{:S(2)}) collective-permute-start(bf16[16,256]{1,0:T(8,128)(2,1)S(1)} %slice_bitcast_fusion), channel_id=1, source_target_pairs={{0,64},{64,0},{128,192},{192,128},{1,65},{65,1},{129,193},{193,129... | collective-permute-start | bytes 24584 | tf_op jit(solution)/shard_map/ppermute | solution.py:405
  87.3 1.2 %collective-permute-done.5 = bf16[16,256]{1,0:T(8,128)(2,1)S(1)} collective-permute-done((bf16[16,256]{1,0:T(8,128)(2,1)S(1)}, bf16[16,256]{1,0:T(8,128)(2,1)S(1)}, u32[]{:S(2)}, u32[]{:S(2)}) %collective-permute-start.5) | collective-permute-done | bytes 8224 | tf_op jit(solution)/shard_map/ppermute | solution.py:405
  88.5 11.3 %all_to_all.17.own = bf16[32,16,256]{2,1,0:T(8,128)(2,1)S(1)} all-to-all(bf16[32,16,256]{2,1,0:T(8,128)(2,1)S(1)} %broadcast_in_dim.29), channel_id=1, replica_groups=mesh['plane'=4,'mode_0'=4,'mode_1'=4,'mode_2'=2,'mode_3'=2] {'mode_0','m..., dimensions={0} | all-to-all | bytes 524288 | tf_op jit(solution)/shard_map/all_to_all | solution.py:409
  99.8 5.2 %collective-permute-start.6 = (bf16[32,16,256]{2,1,0:T(8,128)(2,1)S(1)}, bf16[32,16,256]{2,1,0:T(8,128)(2,1)S(1)}, u32[]{:S(2)}, u32[]{:S(2)}) collective-permute-start(bf16[32,16,256]{2,1,0:T(8,128)(2,1)S(1)} %all_to_all.17.own), channel_id=1, source_target_pairs={{0,1},{1,0},{2,3},{3,2},{4,5},{5,4},{6,7},{7,6},{8,9},{9,8},{10,11... | collective-permute-start | bytes 786440 | tf_op jit(solution)/shard_map/ppermute | solution.py:401
  105.0 1.2 %collective-permute-done.6.other = bf16[32,16,256]{2,1,0:T(8,128)(2,1)S(1)} collective-permute-done((bf16[32,16,256]{2,1,0:T(8,128)(2,1)S(1)}, bf16[32,16,256]{2,1,0:T(8,128)(2,1)S(1)}, u32[]{:S(2)}, u32[]{:S(2)}) %collective-permute-start.6) | collective-permute-done | bytes 262176 | tf_op jit(solution)/shard_map/ppermute | solution.py:401
  106.2 1.3 %finish.1 = f32[1,512,512]{2,1,0:T(8,128)} custom-call(s32[1]{0:T(128)} %bitcast.core_id, f32[1,512,512]{2,1,0:T(8,128)S(1)} %copy-done.1, bf16[32,16,256]{2,1,0:T(8,128)(2,1)S(1)} %all_to_all.17.own, bf16[32,16,256]{2,1,0:T(8,128)(2,1)S(1)} %collective-permute-done.6.other), custom_call_target="tpu_custom_call" | custom-call | tf_op jit(solution)/shard_map/finish/pallas_call | solution.py:390
  (7 shorter events, 0.1 us)
Async XLA Ops:
  0.0 1.2 %copy-start = (f32[1,512,512]{2,1,0:T(8,128)S(1)}, f32[1,512,512]{2,1,0:T(8,128)}, u32[]{:S(2)}) copy-start(f32[1,512,512]{2,1,0:T(8,128)} %phase.5) | copy-start | bytes 3145732
  1.3 5.0 %collective-permute-start = (bf16[16,512]{1,0:T(8,128)(2,1)S(1)}, bf16[16,512]{1,0:T(8,128)(2,1)S(1)}, u32[]{:S(2)}, u32[]{:S(2)}) collective-permute-start(bf16[16,512]{1,0:T(8,128)(2,1)S(1)} %tangent.1), channel_id=1, source_target_pairs={{0,64},{64,0},{128,192},{192,128},{1,65},{65,1},{129,193},{193,129... | collective-permute-start | bytes 49160 | tf_op jit(solution)/shard_map/ppermute | solution.py:405
  6.3 7.6 %collective-permute-start.1 = (bf16[2,16,512]{2,1,0:T(8,128)(2,1)S(1)}, bf16[2,16,512]{2,1,0:T(8,128)(2,1)S(1)}, u32[]{:S(2)}, u32[]{:S(2)}) collective-permute-start(bf16[2,16,512]{2,1,0:T(8,128)(2,1)S(1)} %pad_maximum_fusion.1), channel_id=1, source_target_pairs={{0,128},{64,192},{128,0},{192,64},{1,129},{65,193},{129,1},{193,65... | collective-permute-start | bytes 98312 | tf_op jit(solution)/shard_map/ppermute | solution.py:405
  13.9 21.9 %copy-start.1 = (f32[1,512,512]{2,1,0:T(8,128)S(1)}, f32[1,512,512]{2,1,0:T(8,128)}, u32[]{:S(2)}) copy-start(f32[1,512,512]{2,1,0:T(8,128)} %phase.5) | copy-start | bytes 3145732
  31.4 6.3 %collective-permute-start.2 = (bf16[16,3,16,512]{3,2,1,0:T(8,128)(2,1)S(1)}, bf16[16,3,16,512]{3,2,1,0:T(8,128)(2,1)S(1)}, u32[]{:S(2)}, u32[]{:S(2)}) collective-permute-start(bf16[16,3,16,512]{3,2,1,0:T(8,128)(2,1)S(1)} %all_to_all.15.half_own), channel_id=1, source_target_pairs={{0,1},{1,0},{2,3},{3,2},{4,5},{5,4},{6,7},{7,6},{8,9},{9,8},{10,11... | collective-permute-start | bytes 2359304 | tf_op jit(solution)/shard_map/ppermute | solution.py:401
  37.7 0.7 copy-start.4
  37.7 0.7 copy-start.5
  38.4 1.0 copy-start.2
  39.4 1.0 copy-start.3
  53.9 2.7 %collective-permute-start.3 = (bf16[32,4,16,256]{3,2,1,0:T(8,128)(2,1)S(1)}, bf16[32,4,16,256]{3,2,1,0:T(8,128)(2,1)S(1)}, u32[]{:S(2)}, u32[]{:S(2)}) collective-permute-start(bf16[32,4,16,256]{3,2,1,0:T(8,128)(2,1)S(1)} %get-tuple-element.8), channel_id=1, source_target_pairs={{0,1},{1,0},{2,3},{3,2},{4,5},{5,4},{6,7},{7,6},{8,9},{9,8},{10,11... | collective-permute-start | bytes 3145736 | tf_op jit(solution)/shard_map/ppermute | solution.py:401
  78.2 6.6 %collective-permute-start.4 = (bf16[2,16,256]{2,1,0:T(8,128)(2,1)S(1)}, bf16[2,16,256]{2,1,0:T(8,128)(2,1)S(1)}, u32[]{:S(2)}, u32[]{:S(2)}) collective-permute-start(bf16[2,16,256]{2,1,0:T(8,128)(2,1)S(1)} %slice.17), channel_id=1, source_target_pairs={{0,128},{64,192},{128,0},{192,64},{1,129},{65,193},{129,1},{193,65... | collective-permute-start | bytes 49160 | tf_op jit(solution)/shard_map/ppermute | solution.py:405
  84.8 3.7 %collective-permute-start.5 = (bf16[16,256]{1,0:T(8,128)(2,1)S(1)}, bf16[16,256]{1,0:T(8,128)(2,1)S(1)}, u32[]{:S(2)}, u32[]{:S(2)}) collective-permute-start(bf16[16,256]{1,0:T(8,128)(2,1)S(1)} %slice_bitcast_fusion), channel_id=1, source_target_pairs={{0,64},{64,0},{128,192},{192,128},{1,65},{65,1},{129,193},{193,129... | collective-permute-start | bytes 24584 | tf_op jit(solution)/shard_map/ppermute | solution.py:405
  99.8 6.4 %collective-permute-start.6 = (bf16[32,16,256]{2,1,0:T(8,128)(2,1)S(1)}, bf16[32,16,256]{2,1,0:T(8,128)(2,1)S(1)}, u32[]{:S(2)}, u32[]{:S(2)}) collective-permute-start(bf16[32,16,256]{2,1,0:T(8,128)(2,1)S(1)} %all_to_all.17.own), channel_id=1, source_target_pairs={{0,1},{1,0},{2,3},{3,2},{4,5},{5,4},{6,7},{7,6},{8,9},{9,8},{10,11... | collective-permute-start | bytes 786440 | tf_op jit(solution)/shard_map/ppermute | solution.py:401

commit v3 on v2

--- a/solution.py
+++ b/solution.py
@@ -15,13 +15,15 @@
 MODE = ("mode_0", "mode_1", "mode_2", "mode_3")
 XY = ("mode_0", "mode_1")
 CHIPS = ("mode_0", "mode_1", "mode_2")
+ALL_CHIPS = ("plane", *CHIPS)
 CORE = "mode_3"
-XY_DEVICES = 16
 PLANES = 4
 N = 512
 B = 128
 STRIP = 16
 HALF_STRIPS = N // STRIP // 2
+PIECE = (STRIP, N // 2)
+PIECES = 2 * HALF_STRIPS
 CHIRP_RATE = math.pi / 48.0 * (math.pi / 48.0)
 AMPLITUDE = 12.0
 EPSILON = 1e-06
@@ -30,6 +32,7 @@
 SMEM = pl.BlockSpec(memory_space=pltpu.SMEM)
 VMEM = pl.BlockSpec(memory_space=pltpu.VMEM)
 ANY = pl.BlockSpec(memory_space=pl.ANY)
+HBM = pl.BlockSpec(memory_space=pltpu.HBM)
 
 
 def vmem_limit(mib):
@@ -132,24 +135,31 @@
 
 
 def main_kernel(
-    plane_id, core_id, orders, spots, tan_own, half_own, half_other, left, right, keep, send,
-    psi, source_x, far_x, x_ref, v_ref, y_ref, g_ref, mask_ref, tan_ref, grad, sems,
+    plane_id, core_id, orders_in, spots_in, half_own, half_other, left_in, right_in, keep, send,
+    orders, spots, left, right, psi, source_x, far_x, x_ref, v_ref, y_ref, g_ref, mask_ref, tan_ref, grad, sems,
 ):
     mode, core = plane_id[0], core_id[0]
-    arrivals = [pltpu.make_async_copy(tan_own, tan_ref.at[0], sems.at[0])]
-    for j in range(1, PLANES):
-        for n, (half, at) in enumerate(((half_own, core), (half_other, 1 - core))):
-            arrivals.append(
-                pltpu.make_async_copy(half.at[:, j - 1], tan_ref.at[j, at], sems.at[2 * j + n - 1])
-            )
+    pairs = (
+        (orders_in, orders),
+        (spots_in, spots),
+        (left_in, left),
+        (right_in, right),
+        (half_own, tan_ref.at[core]),
+        (half_other, tan_ref.at[1 - core]),
+    )
+    arrivals = [pltpu.make_async_copy(*pair, sems.at[n]) for n, pair in enumerate(pairs)]
     for copy in arrivals:
         copy.start()
+    for copy in arrivals[:2]:
+        copy.wait()
     hermite_tables(psi)
     source_y = psi[orders[1, mode]]
     row = AMPLITUDE * psi[orders[0, mode]][0:1]
     for k in range(4):
         source_x[k * B : (k + 1) * B, :] = jnp.broadcast_to(row[:, lanes(k)], (B, B)).T
 
+    for copy in arrivals[2:4]:
+        copy.wait()
     spot = spots[mode]
     down = spot_profile(spot // SPOT_SIDE, (N, B), 0)
     zero = jnp.zeros((B, B), F32)
@@ -178,12 +188,13 @@
         return pl.ds(k * B + s * STRIP, STRIP)
 
     def decode(plane, s):
-        slot = mode ^ plane
         for k in range(4):
-            t = tan_ref[slot, k // 2, (k % 2) * (B // STRIP) + s].astype(F32)
-            twice = 2.0 / (1.0 + t * t)
-            mask_ref[plane, 0, rows_of(k, s), :] = (twice - 1.0).astype(BF16)
-            mask_ref[plane, 1, rows_of(k, s), :] = (twice * t).astype(BF16)
+            for h in range(2):
+                cols = slice(h * 2 * B, (h + 1) * 2 * B)
+                t = tan_ref[k // 2, plane, 2 * ((k % 2) * (B // STRIP) + s) + h].astype(F32)
+                twice = 2.0 / (1.0 + t * t)
+                mask_ref[plane, 0, rows_of(k, s), cols] = (twice - 1.0).astype(BF16)
+                mask_ref[plane, 1, rows_of(k, s), cols] = (twice * t).astype(BF16)
 
     def mask_at(plane, k, l, s):
         at = mask_ref.at[plane]
@@ -252,11 +263,11 @@
     def returned(plane, back, k, l, s):
         g = (g_ref[plane, 0, rows_of(k, s), lanes(l)], g_ref[plane, 1, rows_of(k, s), lanes(l)])
         piece = 2 * ((k % 2) * (B // STRIP) + s) + l // 2
-        grad[k // 2, piece, mode ^ plane, :, lanes(l % 2)] = back[0] * g[1] + back[1] * g[0]
+        grad[k // 2, plane, piece, :, lanes(l % 2)] = back[0] * g[1] + back[1] * g[0]
         return mul(back, mask_at(plane, k, l, s)) if plane else None
 
     strips = B // STRIP
-    for copy in arrivals:
+    for copy in arrivals[4:]:
         copy.wait()
     lax.fori_loop(0, strips, first_strip, 0)
     for plane in range(1, PLANES - 1):
@@ -306,15 +317,19 @@
         copy.wait()
 
 
-def main_call(plane_id, core_id, orders, spots, tan_own, half_own, half_other, left, right):
-    pieces = (2 * HALF_STRIPS, PLANES, STRIP, N // 2)
+def main_call(plane_id, core_id, orders, spots, half_own, half_other, left, right):
+    half = (PLANES, PIECES, *PIECE)
     return pl.pallas_call(
         main_kernel,
         name="modes",
-        in_specs=[SMEM, SMEM, SMEM, SMEM, ANY, ANY, ANY, VMEM, VMEM],
+        in_specs=[SMEM, SMEM, HBM, HBM, ANY, ANY, HBM, HBM],
         out_specs=[ANY, ANY],
-        out_shape=[jax.ShapeDtypeStruct(pieces, BF16)] * 2,
+        out_shape=[jax.ShapeDtypeStruct(half, BF16)] * 2,
         scratch_shapes=[
+            pltpu.SMEM((2, PLANES), jnp.int32),
+            pltpu.SMEM((PLANES,), jnp.int32),
+            pltpu.VMEM((4, 2 * B, 2 * B), BF16),
+            pltpu.VMEM((4, 2 * B, 2 * B), BF16),
             pltpu.VMEM((ORDERS, 8, N), F32),
             pltpu.VMEM((N, B), F32),
             pltpu.VMEM((2, N, B), F32),
@@ -323,64 +338,53 @@
             pltpu.VMEM((4, N, 2 * B), BF16),
             pltpu.VMEM((PLANES, 2, N, N), BF16),
             pltpu.VMEM((PLANES, 2, N, N), BF16),
-            pltpu.VMEM((PLANES, 2, HALF_STRIPS, STRIP, N), BF16),
-            pltpu.VMEM((2, *pieces), BF16),
-            pltpu.SemaphoreType.DMA((7,)),
+            pltpu.VMEM((2, *half), BF16),
+            pltpu.VMEM((2, *half), BF16),
+            pltpu.SemaphoreType.DMA((6,)),
         ],
         compiler_params=vmem_limit(26),
-    )(plane_id, core_id, orders, spots, tan_own, half_own, half_other, left, right)
-
-
-def tangent_kernel(where, phase, out, rows, sem):
-    copy = pltpu.make_async_copy(phase.at[0, pl.ds(where[0] * STRIP, STRIP)], rows, sem)
-    copy.start()
-    copy.wait()
+    )(plane_id, core_id, orders, spots, half_own, half_other, left, right)
+
+
+def tangent_kernel(strip_id, side_id, phase, out, rows, sem):
+    for side in range(2):
+
+        @pl.when(side_id[0] == side)
+        def _():
+            at = phase.at[0, pl.ds(strip_id[0] * STRIP, STRIP), side * (N // 2) : (side + 1) * (N // 2)]
+            copy = pltpu.make_async_copy(at, rows, sem)
+            copy.start()
+            copy.wait()
+
     out[...] = half_angle_tangent(rows[...]).astype(BF16)
 
 
-def tangent_call(where, phase_masks):
+def tangent_call(strip_id, side_id, phase_masks):
     return pl.pallas_call(
         tangent_kernel,
         name="tangent",
-        in_specs=[SMEM, pl.BlockSpec(memory_space=pltpu.HBM)],
+        in_specs=[SMEM, SMEM, HBM],
         out_specs=VMEM,
-        out_shape=jax.ShapeDtypeStruct((STRIP, N), BF16),
-        scratch_shapes=[pltpu.VMEM((STRIP, N), F32), pltpu.SemaphoreType.DMA],
-        compiler_params=vmem_limit(4),
-    )(where, phase_masks)
-
-
-def own_tangent_kernel(phase, out):
-    def strip(i, carry):
-        x = phase[0, pl.ds(i * STRIP, STRIP), :]
-        out[i // HALF_STRIPS, i % HALF_STRIPS] = half_angle_tangent(x).astype(BF16)
-        return carry
-
-    lax.fori_loop(0, N // STRIP, strip, 0)
-
-
-def own_tangent_call(phase_masks):
-    return pl.pallas_call(
-        own_tangent_kernel,
-        name="own_tangent",
-        in_specs=[VMEM],
-        out_specs=VMEM,
-        out_shape=jax.ShapeDtypeStruct((2, HALF_STRIPS, STRIP, N), BF16),
-        compiler_params=vmem_limit(6),
-    )(phase_masks)
-
-
-def finish_kernel(core_id, phase, own, other, out):
-    squares = jnp.zeros((STRIP, N // 2), F32)
-    for piece in range(2 * HALF_STRIPS):
+        out_shape=jax.ShapeDtypeStruct(PIECE, BF16),
+        scratch_shapes=[pltpu.VMEM(PIECE, F32), pltpu.SemaphoreType.DMA],
+        compiler_params=vmem_limit(59),
+    )(strip_id, side_id, phase_masks)
+
+
+def finish_kernel(core_id, phase_in, own, other, out, phase, sem):
+    arrival = pltpu.make_async_copy(phase_in, phase, sem)
+    arrival.start()
+    squares = jnp.zeros(PIECE, F32)
+    for piece in range(PIECES):
         for part in (own, other):
             x = part[piece].astype(F32)
             squares += x * x
     mean = 4.0 * jnp.sum(squares, keepdims=True) / (N * N)
     scale = -2.0 * lax.rsqrt(mean + EPSILON)
     core = core_id[0]
+    arrival.wait()
     for part, half in ((own, core), (other, 1 - core)):
-        for piece in range(2 * HALF_STRIPS):
+        for piece in range(PIECES):
             rows = pl.ds(half * (N // 2) + (piece // 2) * STRIP, STRIP)
             cols = slice((piece % 2) * (N // 2), (piece % 2 + 1) * (N // 2))
             out[0, rows, cols] = phase[0, rows, cols] + part[piece].astype(F32) * scale
@@ -390,19 +394,16 @@
     return pl.pallas_call(
         finish_kernel,
         name="finish",
-        in_specs=[SMEM, VMEM, VMEM, VMEM],
+        in_specs=[SMEM, HBM, VMEM, VMEM],
         out_specs=VMEM,
         out_shape=jax.ShapeDtypeStruct((1, N, N), F32),
+        scratch_shapes=[pltpu.VMEM((1, N, N), F32), pltpu.SemaphoreType.DMA],
         compiler_params=vmem_limit(8),
     )(core_id, phase_masks, own, other)
 
 
 def swapped(x):
     return lax.ppermute(x, CORE, [(0, 1), (1, 0)])
-
-
-def from_plane(x, step):
-    return lax.ppermute(x, "plane", [(p, p ^ step) for p in range(PLANES)])
 
 
 def exchanged(x, axes):
@@ -417,21 +418,17 @@
 def shards(phase_masks, hg_orders, spot_index):
     core = lax.axis_index(CORE).astype(jnp.int32)
     plane_id, core_id = lax.axis_index("plane").astype(jnp.int32)[None], core[None]
-    group = core * XY_DEVICES + lax.axis_index(XY).astype(jnp.int32)
-    tangent = tangent_call(group[None], phase_masks)
-    tan_own = own_tangent_call(phase_masks)
-    near = from_plane(tangent, 1)
-    far = from_plane(jnp.stack([tangent, near]), 2)
-    half_own = from_everyone(jnp.concatenate([near[None], far]), XY)
+    strip_id = (core * HALF_STRIPS + lax.axis_index(XY).astype(jnp.int32))[None]
+    side_id = lax.axis_index("mode_2").astype(jnp.int32)[None]
+    half = (PLANES, PIECES, *PIECE)
+    half_own = from_everyone(tangent_call(strip_id, side_id, phase_masks), ALL_CHIPS).reshape(half)
     half_other = swapped(half_own)
     left, right = block_operators()
     keep, send = main_call(
-        plane_id, core_id, hg_orders.T, spot_index, tan_own, half_own, half_other, left, right
+        plane_id, core_id, hg_orders.T, spot_index, half_own, half_other, left, right
     )
-    pair = keep + swapped(send)
-    column = jnp.sum(exchanged(pair, CHIPS).astype(F32), axis=0).astype(BF16)
-    two = column[:2] + from_plane(column[2:], 2)
-    total = two[0] + from_plane(two[1], 1)
+    pair = (keep + swapped(send)).reshape(PLANES * PIECES, *PIECE)
+    total = jnp.sum(exchanged(pair, ALL_CHIPS).astype(F32), axis=0).astype(BF16)
     own = from_everyone(total, CHIPS)
     other = swapped(own)
     return finish_call(core_id, phase_masks, own, other)

time: 108 us -> 125 us (1.16)
  blocking collectives: 49.6 us -> 93.9 us
  starting transfers between devices: 28.2 us -> 6.47 us
  waiting for transfers between devices: 8.66 us -> 5.74 us
  local copies, waits for them, and re-layouts: 4.1 us -> 1.48 us
    all_to_all x3, blocking collectives: 49.6 us -> 93.9 us  [exchanged(): return lax.all_to_all(x, axes, split_axis=0, concat_axis=0, tiled=True)]
    ppermute x4 -> x0, starting transfers between devices: 18.2 us -> none  [from_plane(): return lax.ppermute(x, 'plane', [(p, p ^ step) for p in range(PLANES)])]
    ppermute x4 -> x0, waiting for transfers between devices: 4.74 us -> none  [from_plane(): return lax.ppermute(x, 'plane', [(p, p ^ step) for p in range(PLANES)])]
    ppermute x3, starting transfers between devices: 10 us -> 6.47 us  [swapped(): return lax.ppermute(x, CORE, [(0, 1), (1, 0)])]
    unnamed x12 -> x10, local copies, waits for them, and re-layouts: 3.99 us -> 0.69 us
    ppermute x3, waiting for transfers between devices: 3.92 us -> 5.74 us  [swapped(): return lax.ppermute(x, CORE, [(0, 1), (1, 0)])]
    pallas_call x4 -> x3, Pallas kernels: 16.3 us -> 16.2 us  [the longest x1 13.5 us: main_call(): pl.pallas_call(main_kernel, name='modes', in_specs=[SMEM, SMEM, HBM, HBM,...]
  transfers between devices with their start and end apart: 7 -> 3, of which waited for: 7 -> 3; matrix products, arithmetic and copies ran while one was open for 0% -> 0% of each run, Pallas kernels for 1% -> 0%
where the time goes in v3:
time: 125 us; the launch traced here: 124 us
  blocking collectives  93.9 us (75%)
  Pallas kernels  16.2 us (13%)
  starting transfers between devices  6.47 us (5%)
  waiting for transfers between devices  5.74 us (5%)
  local copies, waits for them, and re-layouts  1.48 us (1%)
    all_to_all x3, blocking collectives, exchanged(): return lax.all_to_all(x, axes, split_axis=0, concat_axis=0, tiled=True)  93.9 us
    pallas_call x1, Pallas kernels, main_call(): pl.pallas_call(main_kernel, name='modes', in_specs=[SMEM, SMEM, HBM, HBM,...  13.5 us
    ppermute x3, starting transfers between devices, swapped(): return lax.ppermute(x, CORE, [(0, 1), (1, 0)])  6.47 us
    ppermute x3, waiting for transfers between devices, swapped(): return lax.ppermute(x, CORE, [(0, 1), (1, 0)])  5.74 us
  transfers between devices with their start and end apart: 3, of which 3 were waited for; matrix products, arithmetic and copies ran while one was open for 0% of the time, Pallas kernels for 0%

profile of v3, /device:TPU:1, one launch (start us, length us, event | category | flops | bytes accessed | tf_op | source)
XLA Modules:
  0.0 124.4 jit_solution(3093376887105279326)
XLA Ops:
  0.0 1.3 %tangent.1 = bf16[16,256]{1,0:T(8,128)(2,1)} custom-call(s32[1]{0:T(128)} %bitcast.3.strip_id, s32[1]{0:T(128)} %bitcast.4.side_id, f32[1,512,512]{2,1,0:T(8,128)} %phase_in.1), custom_call_target="tpu_custom_call" | custom-call | tf_op jit(solution)/shard_map/tangent/pallas_call | solution.py:363
  1.4 0.8 broadcast_in_dim.28
  2.1 0.0 copy-start.1
  2.1 0.0 copy-start.2
  2.2 46.2 %all_to_all.15 = bf16[128,16,256]{2,1,0:T(8,128)(2,1)S(1)} all-to-all(bf16[128,16,256]{2,1,0:T(8,128)(2,1)S(1)} %broadcast_in_dim.28), channel_id=1, replica_groups=mesh['plane'=4,'mode_0'=4,'mode_1'=4,'mode_2'=2,'mode_3'=2] {'plane','mo..., dimensions={0} | all-to-all | bytes 2097152 | tf_op jit(solution)/shard_map/all_to_all | solution.py:410
  48.4 2.7 %collective-permute-start = (bf16[4,32,16,256]{3,2,1,0:T(8,128)(2,1)S(1)}, bf16[4,32,16,256]{3,2,1,0:T(8,128)(2,1)S(1)}, u32[]{:S(2)}, u32[]{:S(2)}) collective-permute-start(bf16[4,32,16,256]{3,2,1,0:T(8,128)(2,1)S(1)} %bitcast.7), channel_id=1, source_target_pairs={{0,1},{1,0},{2,3},{3,2},{4,5},{5,4},{6,7},{7,6},{8,9},{9,8},{10,11... | collective-permute-start | bytes 3145736 | tf_op jit(solution)/shard_map/ppermute | solution.py:406
  51.1 2.3 %collective-permute-done.half_other = bf16[4,32,16,256]{3,2,1,0:T(8,128)(2,1)S(1)} collective-permute-done((bf16[4,32,16,256]{3,2,1,0:T(8,128)(2,1)S(1)}, bf16[4,32,16,256]{3,2,1,0:T(8,128)(2,1)S(1)}, u32[]{:S(2)}, u32[]{:S(2)}) %collective-permute-start) | collective-permute-done | bytes 1048608 | tf_op jit(solution)/shard_map/ppermute | solution.py:406
  53.4 0.0 copy-start.3
  53.4 0.0 copy-start.4
  53.4 0.0 copy-done.1
  53.4 0.0 copy-done.2
  53.4 0.7 copy-done.3
  54.1 0.0 copy-done.4
  54.1 13.5 %modes.1 = (bf16[4,32,16,256]{3,2,1,0:T(8,128)(2,1)S(1)}, bf16[4,32,16,256]{3,2,1,0:T(8,128)(2,1)S(1)}) custom-call(s32[1]{0:T(128)} %bitcast.1.plane_id, s32[1]{0:T(128)} %bitcast.core_id, s32[2,4]{1,0:T(2,128)S(1)} %bitcast.9, s32[4]{0:T(128)S(1)} %copy-done.4, bf16[4,32,16,256]{3,2,1,0:T(8,128)(2,1)S(1)} %bitcast.8, ...), custom_call_target="tpu_custom_call" | custom-call | tf_op jit(solution)/shard_map/modes/pallas_call | solution.py:322
  67.6 0.5 collective-permute-start.1
  68.1 2.3 %collective-permute-done.1 = bf16[4,32,16,256]{3,2,1,0:T(8,128)(2,1)S(1)} collective-permute-done((bf16[4,32,16,256]{3,2,1,0:T(8,128)(2,1)S(1)}, bf16[4,32,16,256]{3,2,1,0:T(8,128)(2,1)S(1)}, u32[]{:S(2)}, u32[]{:S(2)}) %collective-permute-start.1) | collective-permute-done | bytes 1048608 | tf_op jit(solution)/shard_map/ppermute | solution.py:406
  70.4 0.3 add.11
  70.7 36.1 %all_to_all.16 = bf16[128,16,256]{2,1,0:T(8,128)(2,1)S(1)} all-to-all(bf16[128,16,256]{2,1,0:T(8,128)(2,1)S(1)} %bitcast.10), channel_id=1, replica_groups=mesh['plane'=4,'mode_0'=4,'mode_1'=4,'mode_2'=2,'mode_3'=2] {'plane','mo..., dimensions={0} | all-to-all | bytes 2097152 | tf_op jit(solution)/shard_map/all_to_all | solution.py:410
  106.8 0.0 copy-start
  106.9 0.2 reduce_sum.12
  107.1 11.5 %all_to_all.17.own = bf16[32,16,256]{2,1,0:T(8,128)(2,1)S(1)} all-to-all(bf16[32,16,256]{2,1,0:T(8,128)(2,1)S(1)} %broadcast_in_dim.29), channel_id=1, replica_groups=mesh['plane'=4,'mode_0'=4,'mode_1'=4,'mode_2'=2,'mode_3'=2] {'mode_0','m..., dimensions={0} | all-to-all | bytes 524288 | tf_op jit(solution)/shard_map/all_to_all | solution.py:410
  118.6 3.3 %collective-permute-start.2 = (bf16[32,16,256]{2,1,0:T(8,128)(2,1)S(1)}, bf16[32,16,256]{2,1,0:T(8,128)(2,1)S(1)}, u32[]{:S(2)}, u32[]{:S(2)}) collective-permute-start(bf16[32,16,256]{2,1,0:T(8,128)(2,1)S(1)} %all_to_all.17.own), channel_id=1, source_target_pairs={{0,1},{1,0},{2,3},{3,2},{4,5},{5,4},{6,7},{7,6},{8,9},{9,8},{10,11... | collective-permute-start | bytes 786440 | tf_op jit(solution)/shard_map/ppermute | solution.py:406
  121.8 1.2 collective-permute-done.2.other
  123.0 0.0 copy-done
  123.0 1.4 %finish.1 = f32[1,512,512]{2,1,0:T(8,128)} custom-call(s32[1]{0:T(128)} %bitcast.core_id, f32[1,512,512]{2,1,0:T(8,128)S(1)} %copy-done, bf16[32,16,256]{2,1,0:T(8,128)(2,1)S(1)} %all_to_all.17.own, bf16[32,16,256]{2,1,0:T(8,128)(2,1)S(1)} %collective-permute-done.2.other), custom_call_target="tpu_custom_call" | custom-call | tf_op jit(solution)/shard_map/finish/pallas_call | solution.py:394
  (1 shorter events, 0.0 us)
Async XLA Ops:
  2.1 51.3 %copy-start.1 = (bf16[4,256,256]{2,1,0:T(8,128)(2,1)S(1)}, bf16[4,256,256]{2,1,0:T(8,128)(2,1)}, u32[]{:S(2)}) copy-start(bf16[4,256,256]{2,1,0:T(8,128)(2,1)} %constant.36.right_in) | copy-start | bytes 1572868
  2.1 51.3 %copy-start.2 = (bf16[4,256,256]{2,1,0:T(8,128)(2,1)S(1)}, bf16[4,256,256]{2,1,0:T(8,128)(2,1)}, u32[]{:S(2)}) copy-start(bf16[4,256,256]{2,1,0:T(8,128)(2,1)} %constant.35.left_in) | copy-start | bytes 1572868
  48.4 5.0 %collective-permute-start = (bf16[4,32,16,256]{3,2,1,0:T(8,128)(2,1)S(1)}, bf16[4,32,16,256]{3,2,1,0:T(8,128)(2,1)S(1)}, u32[]{:S(2)}, u32[]{:S(2)}) collective-permute-start(bf16[4,32,16,256]{3,2,1,0:T(8,128)(2,1)S(1)} %bitcast.7), channel_id=1, source_target_pairs={{0,1},{1,0},{2,3},{3,2},{4,5},{5,4},{6,7},{7,6},{8,9},{9,8},{10,11... | collective-permute-start | bytes 3145736 | tf_op jit(solution)/shard_map/ppermute | solution.py:406
  53.4 0.7 copy-start.3
  53.4 0.7 copy-start.4
  67.6 2.7 %collective-permute-start.1 = (bf16[4,32,16,256]{3,2,1,0:T(8,128)(2,1)S(1)}, bf16[4,32,16,256]{3,2,1,0:T(8,128)(2,1)S(1)}, u32[]{:S(2)}, u32[]{:S(2)}) collective-permute-start(bf16[4,32,16,256]{3,2,1,0:T(8,128)(2,1)S(1)} %get-tuple-element.8), channel_id=1, source_target_pairs={{0,1},{1,0},{2,3},{3,2},{4,5},{5,4},{6,7},{7,6},{8,9},{9,8},{10,11... | collective-permute-start | bytes 3145736 | tf_op jit(solution)/shard_map/ppermute | solution.py:406
  106.8 16.1 %copy-start = (f32[1,512,512]{2,1,0:T(8,128)S(1)}, f32[1,512,512]{2,1,0:T(8,128)}, u32[]{:S(2)}) copy-start(f32[1,512,512]{2,1,0:T(8,128)} %phase_in.1) | copy-start | bytes 3145732
  118.6 4.4 %collective-permute-start.2 = (bf16[32,16,256]{2,1,0:T(8,128)(2,1)S(1)}, bf16[32,16,256]{2,1,0:T(8,128)(2,1)S(1)}, u32[]{:S(2)}, u32[]{:S(2)}) collective-permute-start(bf16[32,16,256]{2,1,0:T(8,128)(2,1)S(1)} %all_to_all.17.own), channel_id=1, source_target_pairs={{0,1},{1,0},{2,3},{3,2},{4,5},{5,4},{6,7},{7,6},{8,9},{9,8},{10,11... | collective-permute-start | bytes 786440 | tf_op jit(solution)/shard_map/ppermute | solution.py:406
